TPU v7x, 32 devices: a whole 2x2x4 slice. The times are simulated.
32 devices in a mesh: groups: 2 (over y), seq: 4 (over z), head: 4 (over x, core).
Axes of the slice: x: 2, y: 2, z: 4, core: 2. Of those that a mesh axis runs over, the one named last changes fastest.
Arguments:
- query: bfloat16 [16, 1024, 128], P('head', ('groups', 'seq')), parts along dimension 1, may hold values from -400 to 400
- keys: bfloat16 [4, 1024, 128], P('head', ('groups', 'seq')), parts along dimension 1, may hold values from -5 to 5
- values: bfloat16 [4, 1024, 128], P('head', ('groups', 'seq')), parts along dimension 1, may hold values from -6 to 6
- ratio: bfloat16 [16, 1024, 128], P('head', ('groups', 'seq')), parts along dimension 1, may hold values from -4 to 4
- block_order: int32 [16], P('groups'), parts along dimension 0, may hold values from 0 to 7, each once
Outputs:
- query_rel: float32 [16, 1024, 128], P('head', ('groups', 'seq')), parts along dimension 1
- key_rel: float32 [4, 1024, 128], P('head', ('groups', 'seq')), parts along dimension 1
- value_rel: float32 [4, 1024, 128], P('head', ('groups', 'seq')), parts along dimension 1
There are 2 independent parts, one for each index of `groups`. A program takes and returns all parts, laid end to end along the dimension named above; each array names one. Nothing has to cross between parts.
Inputs may be any that keep to these rules, and one draw needn't show every extreme that they name: A permutation: stored block b holds prompt block block_order[b], each once.
All inputs are finite; a program needn't handle non-finite values.
Results may differ from a plain program's by a relative error of at most 0.04.
Values may be sent and summed in bfloat16 or wider, within the bound.
No kernel may reach another device: no remote copies, remote signals or barrier semaphores. Data moves between devices by JAX's collectives and lax.ppermute only.
A program may use at most 64 MiB of HBM per device.

v0:
```python
import functools
import math

import jax
import jax.numpy as jnp
from jax import lax
from jax.experimental import pallas as pl
from jax.experimental.pallas import tpu as pltpu
from jax.sharding import PartitionSpec as P


F32 = jnp.float32
BF16 = jnp.bfloat16
HIDDEN = -1e30
FEW = 8
LOG2E = math.log2(math.e)
KEYS_FIRST = (2, 3, 1)
TERMS_FIRST = (3, 1, 2)


def dot(a, b, dims):
    return lax.dot_general(a, b, (dims, ((), ())), preferred_element_type=F32)


def folded(combine, tile):
    return combine(tile.reshape(tile.shape[0] // 8, 8, tile.shape[1]), axis=0)


def place_limits(shape, order_ref, mine, owner, queries):
    blocks, block_rows = shape
    lane = lax.broadcasted_iota(jnp.int32, (1, queries), 1) % (blocks * block_rows)
    places = lane % block_rows
    for block in range(blocks):
        first = order_ref[mine * blocks + block] * block_rows
        places = places + jnp.where(lane // block_rows == block, first, 0)
    return [places - order_ref[owner * blocks + block] * block_rows for block in range(blocks)]


def masked_scores(limits, query, keys):
    block_rows = keys.shape[0] // len(limits)
    inner = lax.broadcasted_iota(jnp.int32, (block_rows, query.shape[0]), 0)
    found = dot(keys, query, ((1,), (1,)))
    parts = []
    for block, limit in enumerate(limits):
        part = found[block * block_rows : (block + 1) * block_rows]
        parts.append(jnp.where(inner <= limit, part, HIDDEN))
    return jnp.concatenate(parts, axis=0)


def block_softmax(scale, limits, query, ratio, both):
    head = query.shape[1]
    found = masked_scores(limits, query, both[:, :head])
    top = jnp.max(folded(jnp.max, found), axis=0, keepdims=True)
    power = jnp.exp2((found - top) * (scale * LOG2E))
    grad = dot(both[:, head:], ratio, ((1,), (1,)))
    total = jnp.sum(folded(jnp.sum, power), axis=0, keepdims=True)
    weighted = jnp.sum(folded(jnp.sum, power * grad), axis=0, keepdims=True)
    return power, grad, (top, total, weighted)


def store_block(results, power_ref, grad_ref, stat_ref):
    power, grad, stats = results
    power_ref[...] = power
    grad_ref[...] = grad
    for row, stat in enumerate(stats):
        stat_ref[row : row + 1, :] = stat


def own_block_kernel(shape, scale, order_ref, owner_ref, query_ref, ratio_ref, both_ref, *rest):
    *outs, hide_ref = rest
    blocks, queries = shape[0], query_ref.shape[0]
    own = place_limits(shape, order_ref, owner_ref[0], owner_ref[0], queries)
    for slot in range(1, hide_ref.shape[0] // blocks):
        limits = place_limits(shape, order_ref, owner_ref[0], owner_ref[slot], queries)
        for block, limit in enumerate(limits):
            row = slot * blocks + block
            hide_ref[row : row + 1, :] = jnp.where(limit < 0, -HIDDEN, 0.0)
    results = block_softmax(scale, own, query_ref[...], ratio_ref[...], both_ref[...])
    store_block(results, *outs)


def finish(power, grad, share, expect, query, ratio):
    weights = power * share
    soft = (weights * (grad - expect)).astype(BF16)
    key_part = dot(soft, query, ((1,), (0,)))
    value_part = dot(weights.astype(BF16), ratio, ((1,), (0,)))
    return soft, key_part, value_part


def seen_softmax(scale, found, hides, top, grad):
    step = found.shape[0] // len(hides)
    parts = [found[row : row + step] for row in range(0, found.shape[0], step)]
    for part, hide in zip(parts, hides):
        own = jnp.max(folded(jnp.max, part), axis=0, keepdims=True) - hide
        top = jnp.maximum(top, own)
    power = jnp.concatenate(
        [jnp.exp2((part - (top + hide)) * (scale * LOG2E)) for part, hide in zip(parts, hides)],
        axis=0,
    )
    total = jnp.sum(folded(jnp.sum, power), axis=0, keepdims=True)
    weighted = jnp.sum(folded(jnp.sum, power * grad), axis=0, keepdims=True)
    return power, (top, total, weighted)


def block_kernel(blocks, scale, slot, hide_ref, query_ref, ratio_ref, both_ref, power_ref, grad_ref, stat_ref):
    hides = [hide_ref[row : row + 1, :] for row in range(slot * blocks, (slot + 1) * blocks)]
    head = query_ref.shape[1]
    found = dot(both_ref[:, :head], query_ref[...], ((1,), (1,)))
    grad = dot(both_ref[:, head:], ratio_ref[...], ((1,), (1,)))
    least = jnp.full((1, found.shape[1]), 0.1 * HIDDEN, F32)
    power, stats = seen_softmax(scale, found, hides, least, grad)
    store_block((power, grad, stats), power_ref, grad_ref, stat_ref)


def late_kernel(blocks, scale, order, late, width, hide_ref, query_ref, ratio_ref, *rest):
    early = [slot for slot in order if slot not in late]
    seen_refs, rest = rest[: len(late)], rest[len(late) :]
    stat_refs, rest = rest[: len(early) + 1], rest[len(early) + 1 :]
    tile_refs, rest = rest[: 2 * len(early)], rest[2 * len(early) :]
    term_ref, soft_ref, norm_ref, low_ref = rest
    rows = seen_refs[0].shape[0]
    queries, head = query_ref.shape
    keys = jnp.concatenate([ref[:, :head] for ref in seen_refs], axis=0)
    values = jnp.concatenate([ref[:, head:] for ref in seen_refs], axis=0)
    for start in range(0, queries, width):
        span = slice(start, start + width)
        hides = [
            hide_ref[row : row + 1, span]
            for slot in late
            for row in range(slot * blocks, (slot + 1) * blocks)
        ]
        stats = [[ref[row : row + 1, span] for row in range(3)] for ref in stat_refs]
        top = functools.reduce(jnp.maximum, [stat[0] for stat in stats])
        found = dot(keys, query_ref[span, :], ((1,), (1,)))
        grad = dot(values, ratio_ref[span, :], ((1,), (1,)))
        power, (top, total, weighted) = seen_softmax(scale, found, hides, top, grad)
        shares = [jnp.exp2((stat[0] - top) * (scale * LOG2E)) for stat in stats]
        for share, stat in zip(shares, stats):
            total = total + share * stat[1]
            weighted = weighted + share * stat[2]
        whole = 1.0 / total
        expect = weighted * whole
        norm_ref[0:1, span] = shares[0] * whole
        norm_ref[1:2, span] = expect
        for place, slot in enumerate(order):
            if slot in late:
                first = late.index(slot) * rows
                weights = power[first : first + rows] * whole
                slopes = grad[first : first + rows]
            else:
                one = early.index(slot)
                weights = tile_refs[2 * one][:, span] * (shares[one + 1] * whole)
                slopes = tile_refs[2 * one + 1][:, span]
            lines = slice(place * rows, (place + 1) * rows)
            soft_ref[lines, span] = (weights * (slopes - expect)).astype(BF16)
            low_ref[lines, span] = weights.astype(BF16)
    store_terms(soft_ref[:rows], low_ref[:rows], query_ref, ratio_ref, [term_ref])


def store_terms(soft, low, query_ref, ratio_ref, term_refs):
    head = query_ref.shape[1]
    key_part = dot(soft, query_ref[...], ((1,), (0,))).astype(BF16)
    value_part = dot(low, ratio_ref[...], ((1,), (0,))).astype(BF16)
    for place, term_ref in enumerate(term_refs):
        rows = term_ref.shape[0]
        term_ref[:, :head] = key_part[place * rows : (place + 1) * rows]
        term_ref[:, head:] = value_part[place * rows : (place + 1) * rows]


def rest_kernel(query_ref, ratio_ref, soft_ref, low_ref, *term_refs):
    rows = term_refs[0].shape[0]
    store_terms(soft_ref[rows:], low_ref[rows:], query_ref, ratio_ref, term_refs)


def own_kernel(factor, query_ref, ratio_ref, power_ref, grad_ref, norm_ref, both_ref, soft_ref, *rest):
    *seen_refs, own_ref, out_ref = rest
    head = query_ref.shape[1]
    soft, key_part, value_part = finish(
        power_ref[...],
        grad_ref[...],
        norm_ref[0:1, :],
        norm_ref[1:2, :],
        query_ref[...],
        ratio_ref[...],
    )
    own_ref[:, :head] = key_part
    own_ref[:, head:] = value_part
    keys = jnp.concatenate([ref[:, :head] for ref in seen_refs], axis=0)
    found = dot(soft, both_ref[:, :head], ((0,), (0,))) + dot(soft_ref[...], keys, ((0,), (0,)))
    out_ref[...] = factor * query_ref[...].astype(F32) * found


def sum_kernel(factor, both_ref, own_ref, *rest):
    *got, key_out, value_out = rest
    head = key_out.shape[1]
    total = own_ref[...]
    for one in got:
        total = total + one[...].astype(F32)
    key_out[...] = factor * both_ref[:, :head].astype(F32) * total[:, :head]
    value_out[...] = both_ref[:, head:].astype(F32) * total[:, head:]


def whole_kernel(shape, scale, order_ref, owner_ref, query_ref, ratio_ref, seen_ref, terms_ref, out_ref, score_ref, grad_ref):
    slots, blocks, block_rows = shape
    rows = blocks * block_rows
    queries, head = query_ref.shape
    query, ratio = query_ref[...], ratio_ref[...]

    def rows_of(slot):
        return pl.ds(pl.multiple_of(slot * rows, rows), rows)

    def scores(slot, top):
        limits = place_limits((blocks, block_rows), order_ref, owner_ref[0], slot, queries)
        found = masked_scores(limits, query, seen_ref[slot, :, :head])
        score_ref[rows_of(slot), :] = found
        grad_ref[rows_of(slot), :] = dot(seen_ref[slot, :, head:], ratio, ((1,), (1,)))
        return jnp.maximum(top, folded(jnp.max, found))

    top = lax.fori_loop(0, slots, scores, jnp.full((8, queries), HIDDEN, F32))
    top = jnp.max(top, axis=0, keepdims=True)
    zero = jnp.zeros((8, queries), F32)

    def exps(slot, sums):
        power = jnp.exp2((score_ref[rows_of(slot), :] - top) * (scale * LOG2E))
        score_ref[rows_of(slot), :] = power
        weighted = power * grad_ref[rows_of(slot), :]
        return sums[0] + folded(jnp.sum, power), sums[1] + folded(jnp.sum, weighted)

    total, weighted = lax.fori_loop(0, slots, exps, (zero, zero))
    share = 1.0 / jnp.sum(total, axis=0, keepdims=True)
    expect = jnp.sum(weighted, axis=0, keepdims=True) * share
    out_ref[...] = jnp.zeros_like(out_ref)

    def terms(slot, carry):
        soft, key_part, value_part = finish(
            score_ref[rows_of(slot), :], grad_ref[rows_of(slot), :], share, expect, query, ratio
        )
        terms_ref[slot, :, :head] = key_part
        terms_ref[slot, :, head:] = value_part
        out_ref[...] += dot(soft, seen_ref[slot, :, :head], ((0,), (0,)))
        return carry

    lax.fori_loop(0, slots, terms, 0)
    out_ref[...] = 0.5 * scale * query.astype(F32) * out_ref[...]


def body(query, keys, values, ratio, block_order):
    kv_heads, rows, head = keys.shape
    group = query.shape[0] // kv_heads
    queries = group * rows
    scale = head ** (-0.5)
    slots = lax.axis_size("seq")
    mine = lax.axis_index("seq")
    blocks = block_order.shape[0] // slots
    block_rows = rows // blocks
    shape = (blocks, block_rows)
    swap = slots & (slots - 1) == 0
    limit = min(60 << 20, (8 << 20) + 16 * slots * rows * queries)
    params = pltpu.CompilerParams(vmem_limit_bytes=limit)
    smem = pl.BlockSpec(memory_space=pltpu.SMEM)
    vmem = pl.BlockSpec(memory_space=pltpu.VMEM)
    tile = jax.ShapeDtypeStruct((rows, queries), F32)
    stat = jax.ShapeDtypeStruct((8, queries), F32)
    low_term = jax.ShapeDtypeStruct((rows, 2 * head), BF16)
    term = jax.ShapeDtypeStruct((rows, 2 * head), F32)
    part = jax.ShapeDtypeStruct((rows, head), F32)
    rel = jax.ShapeDtypeStruct((queries, head), F32)

    def run(kernel, outs, scalars, arrays, dots, scratch=()):
        single = not isinstance(outs, tuple)
        return pl.pallas_call(
            kernel,
            out_shape=outs,
            in_specs=[smem] * len(scalars) + [vmem] * len(arrays),
            out_specs=vmem if single else (vmem,) * len(outs),
            scratch_shapes=scratch,
            compiler_params=params,
            cost_estimate=pl.CostEstimate(
                flops=2 * dots * rows * queries * head,
                bytes_accessed=4 * dots * rows * queries,
                transcendentals=rows * queries,
            ),
        )(*scalars, *arrays)

    def pairs(step, back):
        if swap:
            return [(device, device ^ step) for device in range(slots)]
        step = -step if back else step
        return [(device, (device + step) % slots) for device in range(slots)]

    def many(query_rows, ratio_rows, both):
        seen = lax.all_gather(both, "seq")
        terms, query_out = run(
            functools.partial(whole_kernel, (slots, *shape), scale),
            (jax.ShapeDtypeStruct((slots, rows, 2 * head), F32), rel),
            (block_order, mine.reshape(1)),
            (query_rows, ratio_rows, seen),
            5 * slots,
            [pltpu.VMEM((slots * rows, queries), F32)] * 2,
        )
        own = lax.psum_scatter(terms, "seq", scatter_dimension=0, tiled=False)
        return own, [], query_out

    def few(query_rows, ratio_rows, both):
        steps = range(1, slots)
        first = KEYS_FIRST if slots == len(KEYS_FIRST) + 1 else tuple(steps)
        then = TERMS_FIRST if slots == len(TERMS_FIRST) + 1 else tuple(steps)
        seen = {0: both}
        for step in first:
            seen[step] = lax.ppermute(both, "seq", pairs(step, False))
        device = jnp.arange(slots, dtype=jnp.int32)
        owners = mine ^ device if swap else lax.rem(mine - device + slots, slots)
        power, grad, stats = {}, {}, {}
        power[0], grad[0], stats[0], hides = run(
            functools.partial(own_block_kernel, shape, scale),
            (tile, tile, stat, jax.ShapeDtypeStruct((slots * blocks, queries), F32)),
            (block_order, owners),
            (query_rows, ratio_rows, both),
            2,
        )
        width = math.gcd(queries, 256)
        got = []
        early = [slot for slot in then if slot == first[0]]
        late = [slot for slot in then if slot not in early]
        for slot in early:
            power[slot], grad[slot], stats[slot] = run(
                functools.partial(block_kernel, blocks, scale, slot),
                (tile, tile, stat),
                (),
                (hides, query_rows, ratio_rows, seen[slot]),
                2,
            )
        low_tiles = jax.ShapeDtypeStruct((len(then) * rows, queries), BF16)
        term_first, soft, norm, low = run(
            functools.partial(late_kernel, blocks, scale, then, late, width),
            (low_term, low_tiles, stat, low_tiles),
            (),
            (
                *(hides, query_rows, ratio_rows),
                *(seen[slot] for slot in late),
                *(stats[slot] for slot in (0, *early)),
                *(one for slot in early for one in (power[slot], grad[slot])),
            ),
            4 * len(then),
        )
        terms = [term_first]
        if then[1:]:
            terms += run(
                rest_kernel,
                (low_term,) * len(then[1:]),
                (),
                (query_rows, ratio_rows, soft, low),
                2 * len(then[1:]),
            )
        for slot, one in zip(then, terms):
            got.append(lax.ppermute(one, "seq", pairs(slot, True)))
        own, query_out = run(
            functools.partial(own_kernel, 0.5 * scale),
            (term, rel),
            (),
            (
                *(query_rows, ratio_rows, power[0], grad[0], norm, both, soft),
                *(seen[slot] for slot in then),
            ),
            2 + slots,
        )
        return own, got, query_out

    def one_head(query_rows, ratio_rows, key_rows, value_rows):
        both = jnp.concatenate((key_rows, value_rows), axis=1)
        own, got, query_out = (many if slots > FEW else few)(query_rows, ratio_rows, both)
        key_out, value_out = run(
            functools.partial(sum_kernel, 0.5 * scale), (part, part), (), (both, own, *got), 0
        )
        return query_out.reshape(group, rows, head), key_out, value_out

    results = [
        one_head(
            query[g * group : (g + 1) * group].reshape(queries, head),
            ratio[g * group : (g + 1) * group].reshape(queries, head),
            keys[g],
            values[g],
        )
        for g in range(kv_heads)
    ]
    return (
        jnp.concatenate([one for one, _, _ in results], axis=0),
        jnp.stack([one for _, one, _ in results], axis=0),
        jnp.stack([one for _, _, one in results], axis=0),
    )


def solution(mesh):
    spec = P("head", ("groups", "seq"), None)
    return jax.shard_map(
        body,
        mesh=mesh,
        in_specs=(spec, spec, spec, spec, P("groups")),
        out_specs=(spec, spec, spec),
        check_vma=False,
    )
```

profile of v0, /device:TPU:0, one launch (start us, length us, event | category | flops | bytes accessed | tf_op | source)
XLA Modules:
  0.0 23.0 jit_solution(11889866019581165263)
XLA Ops:
  0.6 0.0 copy-start
  0.6 0.8 %pad_maximum_fusion.both_ref = bf16[128,256]{1,0:T(8,128)(2,1)S(1)} fusion(bf16[128,128]{1,0:T(8,128)(2,1)} %bitcast.17, bf16[128,128]{1,0:T(8,128)(2,1)} %bitcast.18), kind=kLoop, calls=%fused_computation | loop fusion | flops 131072 | bytes 131072 | tf_op jit(solution)/shard_map/concatenate | solution.py:370
  1.5 4.1 %collective-permute-start.2 = (bf16[128,256]{1,0:T(8,128)(2,1)S(1)}, bf16[128,256]{1,0:T(8,128)(2,1)S(1)}, u32[]{:S(2)}, u32[]{:S(2)}) collective-permute-start(bf16[128,256]{1,0:T(8,128)(2,1)S(1)} %pad_maximum_fusion.both_ref), channel_id=1, source_target_pairs={{0,8},{4,12},{8,0},{12,4},{1,9},{5,13},{9,1},{13,5},{2,10},{6,14},... | collective-permute-start | bytes 196616 | tf_op jit(solution)/shard_map/ppermute | solution.py:310
  5.6 1.6 %collective-permute-start.1 = (bf16[128,256]{1,0:T(8,128)(2,1)S(1)}, bf16[128,256]{1,0:T(8,128)(2,1)S(1)}, u32[]{:S(2)}, u32[]{:S(2)}) collective-permute-start(bf16[128,256]{1,0:T(8,128)(2,1)S(1)} %pad_maximum_fusion.both_ref), channel_id=1, source_target_pairs={{0,4},{4,0},{8,12},{12,8},{1,5},{5,1},{9,13},{13,9},{2,6},{6,2},{1... | collective-permute-start | bytes 196616 | tf_op jit(solution)/shard_map/ppermute | solution.py:310
  7.2 0.0 collective-permute-start
  7.2 0.0 copy-start.2
  7.2 0.0 copy-done
  7.2 0.6 %copy-done.2 = s32[8]{0:T(128)S(1)} copy-done((s32[8]{0:T(128)S(1)}, s32[8]{0:T(128)}, u32[]{:S(2)}) %copy-start.2) | copy-done | bytes 56
  7.8 0.0 copy-start.1
  7.8 0.9 %copy-done.1 = bf16[4,128,128]{2,1,0:T(8,128)(2,1)S(1)} copy-done((bf16[4,128,128]{2,1,0:T(8,128)(2,1)S(1)}, bf16[4,128,128]{2,1,0:T(8,128)(2,1)}, u32[]{:S(2)}) %copy-start.1) | copy-done | bytes 131096
  8.7 0.8 %shard_map.76 = (f32[128,512]{1,0:T(8,128)S(1)}, f32[128,512]{1,0:T(8,128)S(1)}, f32[8,512]{1,0:T(8,128)S(1)}, f32[8,512]{1,0:T(8,128)S(1)}) custom-call(s32[8]{0:T(128)S(1)} %copy-done.2, s32[4]{0:T(128)S(1)} %iota_xor_fusion.owner_ref, bf16[512,128]{1,0:T(8,128)(2,1)S(1)} %bitcast.7, bf16[512,128]{1,0:T(8,128)(2,1)S(1)} %bitcast.12, ...), custom_call_target="tpu_custom_call" | custom-call | flops 33554432 | bytes 524288 | tf_op jit(solution)/shard_map/pallas_call | solution.py:271
  9.6 0.0 collective-permute-done.2.both_ref.rest_2_
  9.6 0.3 %shard_map.77 = (f32[128,512]{1,0:T(8,128)S(1)}, f32[128,512]{1,0:T(8,128)S(1)}, f32[8,512]{1,0:T(8,128)S(1)}) custom-call(f32[8,512]{1,0:T(8,128)S(1)} %get-tuple-element.22.hide_ref, bf16[512,128]{1,0:T(8,128)(2,1)S(1)} %bitcast.8, bf16[512,128]{1,0:T(8,128)(2,1)S(1)} %bitcast.13, bf16[128,256]{1,0:T(8,128)(2,1)S(1)} %collective-permute-done.2.both_ref.rest_2_), custom_call_target="tpu_custom_call" | custom-call | flops 33554432 | bytes 524288 | tf_op jit(solution)/shard_map/pallas_call | solution.py:271
  9.9 0.0 collective-permute-done.1.rest_1_
  9.9 3.4 %collective-permute-done.rest_0_ = bf16[128,256]{1,0:T(8,128)(2,1)S(1)} collective-permute-done((bf16[128,256]{1,0:T(8,128)(2,1)S(1)}, bf16[128,256]{1,0:T(8,128)(2,1)S(1)}, u32[]{:S(2)}, u32[]{:S(2)}) %collective-permute-start) | collective-permute-done | bytes 65568 | tf_op jit(solution)/shard_map/ppermute | solution.py:310
  13.2 0.7 %shard_map.78 = (bf16[128,256]{1,0:T(8,128)(2,1)S(1)}, bf16[384,512]{1,0:T(8,128)(2,1)S(1)}, f32[8,512]{1,0:T(8,128)S(1)}, bf16[384,512]{1,0:T(8,128)(2,1)S(1)}) custom-call(f32[8,512]{1,0:T(8,128)S(1)} %get-tuple-element.22.hide_ref, bf16[512,128]{1,0:T(8,128)(2,1)S(1)} %bitcast.9, bf16[512,128]{1,0:T(8,128)(2,1)S(1)} %bitcast.14, ...), custom_call_target="tpu_custom_call" | custom-call | flops 201326592 | bytes 3145728 | tf_op jit(solution)/shard_map/pallas_call | solution.py:271
  13.9 0.3 %shard_map.80 = (bf16[128,256]{1,0:T(8,128)(2,1)S(1)}, bf16[128,256]{1,0:T(8,128)(2,1)S(1)}) custom-call(bf16[512,128]{1,0:T(8,128)(2,1)S(1)} %bitcast.10, bf16[512,128]{1,0:T(8,128)(2,1)S(1)} %bitcast.15, bf16[384,512]{1,0:T(8,128)(2,1)S(1)} %get-tuple-element.28.soft_ref, bf16[384,512]{1,0:T(8,128)(2,1)S(1)} %get-tuple-element.32.low_ref), custom_call_target="tpu_custom_call" | custom-call | flops 67108864 | bytes 1048576 | tf_op jit(solution)/shard_map/pallas_call | solution.py:271
  14.2 0.1 collective-permute-start.4
  14.3 1.8 %collective-permute-start.5 = (bf16[128,256]{1,0:T(8,128)(2,1)S(1)}, bf16[128,256]{1,0:T(8,128)(2,1)S(1)}, u32[]{:S(2)}, u32[]{:S(2)}) collective-permute-start(bf16[128,256]{1,0:T(8,128)(2,1)S(1)} %get-tuple-element.34), channel_id=1, source_target_pairs={{0,8},{4,12},{8,0},{12,4},{1,9},{5,13},{9,1},{13,5},{2,10},{6,14},... | collective-permute-start | bytes 196616 | tf_op jit(solution)/shard_map/ppermute | solution.py:356
  16.1 2.6 %collective-permute-start.3 = (bf16[128,256]{1,0:T(8,128)(2,1)S(1)}, bf16[128,256]{1,0:T(8,128)(2,1)S(1)}, u32[]{:S(2)}, u32[]{:S(2)}) collective-permute-start(bf16[128,256]{1,0:T(8,128)(2,1)S(1)} %get-tuple-element.31), channel_id=1, source_target_pairs={{0,12},{4,8},{8,4},{12,0},{1,13},{5,9},{9,5},{13,1},{2,14},{6,10},... | collective-permute-start | bytes 196616 | tf_op jit(solution)/shard_map/ppermute | solution.py:356
  18.7 1.1 %shard_map.79 = (f32[128,256]{1,0:T(8,128)S(1)}, f32[512,128]{1,0:T(8,128)}) custom-call(bf16[512,128]{1,0:T(8,128)(2,1)S(1)} %bitcast.11, bf16[512,128]{1,0:T(8,128)(2,1)S(1)} %bitcast.16, f32[128,512]{1,0:T(8,128)S(1)} %get-tuple-element.20.power_ref, f32[128,512]{1,0:T(8,128)S(1)} %get-tuple-element.21.grad_ref, f32[8,512]{1,0:T(8,128)S(1)} %get-tuple-element.27.norm_ref, ...), custom_call_target="tpu_custom_call" | custom-call | flops 100663296 | bytes 1572864 | tf_op jit(solution)/shard_map/pallas_call | solution.py:271
  19.8 0.0 collective-permute-done.4.rest_1_
  19.8 2.5 %collective-permute-done.5.rest_2_ = bf16[128,256]{1,0:T(8,128)(2,1)S(1)} collective-permute-done((bf16[128,256]{1,0:T(8,128)(2,1)S(1)}, bf16[128,256]{1,0:T(8,128)(2,1)S(1)}, u32[]{:S(2)}, u32[]{:S(2)}) %collective-permute-start.5) | collective-permute-done | bytes 65568 | tf_op jit(solution)/shard_map/ppermute | solution.py:356
  22.3 0.0 collective-permute-done.3.rest_0_
  22.3 0.7 %shard_map.81 = (f32[128,128]{1,0:T(8,128)}, f32[128,128]{1,0:T(8,128)}) custom-call(bf16[128,256]{1,0:T(8,128)(2,1)S(1)} %pad_maximum_fusion.both_ref, f32[128,256]{1,0:T(8,128)S(1)} %get-tuple-element.30.own_ref, bf16[128,256]{1,0:T(8,128)(2,1)S(1)} %collective-permute-done.3.rest_0_, bf16[128,256]{1,0:T(8,128)(2,1)S(1)} %collective-permute-done.4.rest_1_, ...), custom_call_target="tpu_custom_call" | custom-call | tf_op jit(solution)/shard_map/pallas_call | solution.py:271
  (1 shorter events, 0.0 us)
Async XLA Ops:
  0.6 6.5 %copy-start = (bf16[4,128,128]{2,1,0:T(8,128)(2,1)S(1)}, bf16[4,128,128]{2,1,0:T(8,128)(2,1)}, u32[]{:S(2)}) copy-start(bf16[4,128,128]{2,1,0:T(8,128)(2,1)} %param.5) | copy-start | bytes 393220
  1.5 8.1 %collective-permute-start.2 = (bf16[128,256]{1,0:T(8,128)(2,1)S(1)}, bf16[128,256]{1,0:T(8,128)(2,1)S(1)}, u32[]{:S(2)}, u32[]{:S(2)}) collective-permute-start(bf16[128,256]{1,0:T(8,128)(2,1)S(1)} %pad_maximum_fusion.both_ref), channel_id=1, source_target_pairs={{0,8},{4,12},{8,0},{12,4},{1,9},{5,13},{9,1},{13,5},{2,10},{6,14},... | collective-permute-start | bytes 196616 | tf_op jit(solution)/shard_map/ppermute | solution.py:310
  5.6 4.3 %collective-permute-start.1 = (bf16[128,256]{1,0:T(8,128)(2,1)S(1)}, bf16[128,256]{1,0:T(8,128)(2,1)S(1)}, u32[]{:S(2)}, u32[]{:S(2)}) collective-permute-start(bf16[128,256]{1,0:T(8,128)(2,1)S(1)} %pad_maximum_fusion.both_ref), channel_id=1, source_target_pairs={{0,4},{4,0},{8,12},{12,8},{1,5},{5,1},{9,13},{13,9},{2,6},{6,2},{1... | collective-permute-start | bytes 196616 | tf_op jit(solution)/shard_map/ppermute | solution.py:310
  7.2 6.1 %collective-permute-start = (bf16[128,256]{1,0:T(8,128)(2,1)S(1)}, bf16[128,256]{1,0:T(8,128)(2,1)S(1)}, u32[]{:S(2)}, u32[]{:S(2)}) collective-permute-start(bf16[128,256]{1,0:T(8,128)(2,1)S(1)} %pad_maximum_fusion.both_ref), channel_id=1, source_target_pairs={{0,12},{4,8},{8,4},{12,0},{1,13},{5,9},{9,5},{13,1},{2,14},{6,10},... | collective-permute-start | bytes 196616 | tf_op jit(solution)/shard_map/ppermute | solution.py:310
  7.2 0.7 %copy-start.2 = (s32[8]{0:T(128)S(1)}, s32[8]{0:T(128)}, u32[]{:S(2)}) copy-start(s32[8]{0:T(128)} %order_ref.1) | copy-start | bytes 100
  7.8 0.9 %copy-start.1 = (bf16[4,128,128]{2,1,0:T(8,128)(2,1)S(1)}, bf16[4,128,128]{2,1,0:T(8,128)(2,1)}, u32[]{:S(2)}) copy-start(bf16[4,128,128]{2,1,0:T(8,128)(2,1)} %param.8) | copy-start | bytes 393220
  14.2 5.5 %collective-permute-start.4 = (bf16[128,256]{1,0:T(8,128)(2,1)S(1)}, bf16[128,256]{1,0:T(8,128)(2,1)S(1)}, u32[]{:S(2)}, u32[]{:S(2)}) collective-permute-start(bf16[128,256]{1,0:T(8,128)(2,1)S(1)} %get-tuple-element.33), channel_id=1, source_target_pairs={{0,4},{4,0},{8,12},{12,8},{1,5},{5,1},{9,13},{13,9},{2,6},{6,2},{1... | collective-permute-start | bytes 196616 | tf_op jit(solution)/shard_map/ppermute | solution.py:356
  14.3 8.0 %collective-permute-start.5 = (bf16[128,256]{1,0:T(8,128)(2,1)S(1)}, bf16[128,256]{1,0:T(8,128)(2,1)S(1)}, u32[]{:S(2)}, u32[]{:S(2)}) collective-permute-start(bf16[128,256]{1,0:T(8,128)(2,1)S(1)} %get-tuple-element.34), channel_id=1, source_target_pairs={{0,8},{4,12},{8,0},{12,4},{1,9},{5,13},{9,1},{13,5},{2,10},{6,14},... | collective-permute-start | bytes 196616 | tf_op jit(solution)/shard_map/ppermute | solution.py:356
  16.1 6.2 %collective-permute-start.3 = (bf16[128,256]{1,0:T(8,128)(2,1)S(1)}, bf16[128,256]{1,0:T(8,128)(2,1)S(1)}, u32[]{:S(2)}, u32[]{:S(2)}) collective-permute-start(bf16[128,256]{1,0:T(8,128)(2,1)S(1)} %get-tuple-element.31), channel_id=1, source_target_pairs={{0,12},{4,8},{8,4},{12,0},{1,13},{5,9},{9,5},{13,1},{2,14},{6,10},... | collective-permute-start | bytes 196616 | tf_op jit(solution)/shard_map/ppermute | solution.py:356
where the time goes:
time: 23.2 us; the launch traced here: 23 us
  starting transfers between devices  10.1 us (44%)
  waiting for transfers between devices  5.92 us (26%)
  Pallas kernels  3.85 us (17%)
  local copies, waits for them, and re-layouts  1.55 us (7%)
  other arithmetic  0.82 us (4%)
  between operations  0.71 us (3%)
    ppermute x3, starting transfers between devices, few(): seen[step] = lax.ppermute(both, 'seq', pairs(step, False))  5.7 us
    ppermute x3, starting transfers between devices, few(): got.append(lax.ppermute(one, 'seq', pairs(slot, True)))  4.44 us
    pallas_call x6, Pallas kernels, run(): pl.pallas_call(kernel, out_shape=outs, in_specs=[smem] * len(scalars) + [...  3.85 us
    ppermute x3, waiting for transfers between devices, few(): seen[step] = lax.ppermute(both, 'seq', pairs(step, False))  3.37 us
    ppermute x3, waiting for transfers between devices, few(): got.append(lax.ppermute(one, 'seq', pairs(slot, True)))  2.55 us
    unnamed x6, local copies, waits for them, and re-layouts  1.55 us
    concatenate x1, other arithmetic, one_head(): both = jnp.concatenate((key_rows, value_rows), axis=1)  0.82 us
  transfers between devices with their start and end apart: 6, of which 2 were waited for; matrix products, arithmetic and copies ran while one was open for 0% of the time, Pallas kernels for 9%

commit v1 on v0

--- a/solution.py
+++ b/solution.py
@@ -117,7 +117,7 @@
     seen_refs, rest = rest[: len(late)], rest[len(late) :]
     stat_refs, rest = rest[: len(early) + 1], rest[len(early) + 1 :]
     tile_refs, rest = rest[: 2 * len(early)], rest[2 * len(early) :]
-    term_ref, soft_ref, norm_ref, low_ref = rest
+    *term_refs, soft_ref, norm_ref, low_ref = rest
     rows = seen_refs[0].shape[0]
     queries, head = query_ref.shape
     keys = jnp.concatenate([ref[:, :head] for ref in seen_refs], axis=0)
@@ -154,22 +154,11 @@
             lines = slice(place * rows, (place + 1) * rows)
             soft_ref[lines, span] = (weights * (slopes - expect)).astype(BF16)
             low_ref[lines, span] = weights.astype(BF16)
-    store_terms(soft_ref[:rows], low_ref[:rows], query_ref, ratio_ref, [term_ref])
-
-
-def store_terms(soft, low, query_ref, ratio_ref, term_refs):
-    head = query_ref.shape[1]
-    key_part = dot(soft, query_ref[...], ((1,), (0,))).astype(BF16)
-    value_part = dot(low, ratio_ref[...], ((1,), (0,))).astype(BF16)
+    key_part = dot(soft_ref[...], query_ref[...], ((1,), (0,))).astype(BF16)
+    value_part = dot(low_ref[...], ratio_ref[...], ((1,), (0,))).astype(BF16)
     for place, term_ref in enumerate(term_refs):
-        rows = term_ref.shape[0]
         term_ref[:, :head] = key_part[place * rows : (place + 1) * rows]
         term_ref[:, head:] = value_part[place * rows : (place + 1) * rows]
-
-
-def rest_kernel(query_ref, ratio_ref, soft_ref, low_ref, *term_refs):
-    rows = term_refs[0].shape[0]
-    store_terms(soft_ref[rows:], low_ref[rows:], query_ref, ratio_ref, term_refs)
 
 
 def own_kernel(factor, query_ref, ratio_ref, power_ref, grad_ref, norm_ref, both_ref, soft_ref, *rest):
@@ -190,14 +179,33 @@
     out_ref[...] = factor * query_ref[...].astype(F32) * found
 
 
-def sum_kernel(factor, both_ref, own_ref, *rest):
-    *got, key_out, value_out = rest
-    head = key_out.shape[1]
+def presum_kernel(own_ref, *rest):
+    *got, out_ref = rest
     total = own_ref[...]
     for one in got:
         total = total + one[...].astype(F32)
-    key_out[...] = factor * both_ref[:, :head].astype(F32) * total[:, :head]
-    value_out[...] = both_ref[:, head:].astype(F32) * total[:, head:]
+    out_ref[...] = total
+
+
+def sum_kernel(factor, both_ref, own_ref, *rest):
+    *got, key_out, value_out, key_ref, value_ref, sems = rest
+    head = key_out.shape[1]
+    copies = (
+        pltpu.make_async_copy(key_ref, key_out, sems.at[0]),
+        pltpu.make_async_copy(value_ref, value_out, sems.at[1]),
+    )
+    key_part = own_ref[:, :head]
+    for one in got:
+        key_part = key_part + one[:, :head].astype(F32)
+    key_ref[...] = factor * both_ref[:, :head].astype(F32) * key_part
+    copies[0].start()
+    value_part = own_ref[:, head:]
+    for one in got:
+        value_part = value_part + one[:, head:].astype(F32)
+    value_ref[...] = both_ref[:, head:].astype(F32) * value_part
+    copies[1].start()
+    copies[0].wait()
+    copies[1].wait()
 
 
 def whole_kernel(shape, scale, order_ref, owner_ref, query_ref, ratio_ref, seen_ref, terms_ref, out_ref, score_ref, grad_ref):
@@ -266,13 +274,14 @@
     part = jax.ShapeDtypeStruct((rows, head), F32)
     rel = jax.ShapeDtypeStruct((queries, head), F32)
 
-    def run(kernel, outs, scalars, arrays, dots, scratch=()):
+    def run(kernel, outs, scalars, arrays, dots, scratch=(), out_space=pltpu.VMEM):
         single = not isinstance(outs, tuple)
+        space = pl.BlockSpec(memory_space=out_space)
         return pl.pallas_call(
             kernel,
             out_shape=outs,
             in_specs=[smem] * len(scalars) + [vmem] * len(arrays),
-            out_specs=vmem if single else (vmem,) * len(outs),
+            out_specs=space if single else (space,) * len(outs),
             scratch_shapes=scratch,
             compiler_params=params,
             cost_estimate=pl.CostEstimate(
@@ -330,10 +339,13 @@
                 (hides, query_rows, ratio_rows, seen[slot]),
                 2,
             )
-        low_tiles = jax.ShapeDtypeStruct((len(then) * rows, queries), BF16)
-        term_first, soft, norm, low = run(
+        *terms, soft, norm = run(
             functools.partial(late_kernel, blocks, scale, then, late, width),
-            (low_term, low_tiles, stat, low_tiles),
+            (
+                *[low_term] * len(then),
+                jax.ShapeDtypeStruct((len(then) * rows, queries), BF16),
+                stat,
+            ),
             (),
             (
                 *(hides, query_rows, ratio_rows),
@@ -342,16 +354,8 @@
                 *(one for slot in early for one in (power[slot], grad[slot])),
             ),
             4 * len(then),
-        )
-        terms = [term_first]
-        if then[1:]:
-            terms += run(
-                rest_kernel,
-                (low_term,) * len(then[1:]),
-                (),
-                (query_rows, ratio_rows, soft, low),
-                2 * len(then[1:]),
-            )
+            [pltpu.VMEM((len(then) * rows, queries), BF16)],
+        )
         for slot, one in zip(then, terms):
             got.append(lax.ppermute(one, "seq", pairs(slot, True)))
         own, query_out = run(
@@ -364,13 +368,21 @@
             ),
             2 + slots,
         )
-        return own, got, query_out
+        if got[1:]:
+            own = run(presum_kernel, term, (), (own, *got[:-1]), 1)
+        return own, got[-1:], query_out
 
     def one_head(query_rows, ratio_rows, key_rows, value_rows):
         both = jnp.concatenate((key_rows, value_rows), axis=1)
         own, got, query_out = (many if slots > FEW else few)(query_rows, ratio_rows, both)
         key_out, value_out = run(
-            functools.partial(sum_kernel, 0.5 * scale), (part, part), (), (both, own, *got), 0
+            functools.partial(sum_kernel, 0.5 * scale),
+            (part, part),
+            (),
+            (both, own, *got),
+            0,
+            [pltpu.VMEM((rows, head), F32)] * 2 + [pltpu.SemaphoreType.DMA((2,))],
+            out_space=pltpu.HBM,
         )
         return query_out.reshape(group, rows, head), key_out, value_out
 

time: 23.2 us -> 22.9 us (0.987)
  transfers between devices with their start and end apart: 6 -> 6, of which waited for: 2 -> 4; matrix products, arithmetic and copies ran while one was open for 0% -> 0% of each run, Pallas kernels for 9% -> 10%
where the time goes in v1:
time: 22.9 us; the launch traced here: 22.8 us
  starting transfers between devices  10.2 us (45%)
  waiting for transfers between devices  5.92 us (26%)
  Pallas kernels  3.63 us (16%)
  local copies, waits for them, and re-layouts  1.55 us (7%)
  other arithmetic  0.82 us (4%)
  between operations  0.7 us (3%)
    ppermute x3, starting transfers between devices, few(): seen[step] = lax.ppermute(both, 'seq', pairs(step, False))  5.7 us
    ppermute x3, starting transfers between devices, few(): got.append(lax.ppermute(one, 'seq', pairs(slot, True)))  4.45 us
    pallas_call x6, Pallas kernels, run(): pl.pallas_call(kernel, out_shape=outs, in_specs=[smem] * len(scalars) + [...  3.63 us
    ppermute x3, waiting for transfers between devices, few(): seen[step] = lax.ppermute(both, 'seq', pairs(step, False))  3.37 us
    ppermute x3, waiting for transfers between devices, few(): got.append(lax.ppermute(one, 'seq', pairs(slot, True)))  2.55 us
    unnamed x6, local copies, waits for them, and re-layouts  1.55 us
    concatenate x1, other arithmetic, one_head(): both = jnp.concatenate((key_rows, value_rows), axis=1)  0.82 us
  transfers between devices with their start and end apart: 6, of which 4 were waited for; matrix products, arithmetic and copies ran while one was open for 0% of the time, Pallas kernels for 10%

profile of v1, /device:TPU:0, one launch (start us, length us, event | category | flops | bytes accessed | tf_op | source)
XLA Modules:
  0.0 22.8 jit_solution(5913329475031371664)
XLA Ops:
  0.6 0.0 copy-start
  0.6 0.8 %pad_maximum_fusion.both_ref = bf16[128,256]{1,0:T(8,128)(2,1)S(1)} fusion(bf16[128,128]{1,0:T(8,128)(2,1)} %bitcast.15, bf16[128,128]{1,0:T(8,128)(2,1)} %bitcast.16), kind=kLoop, calls=%fused_computation | loop fusion | flops 131072 | bytes 131072 | tf_op jit(solution)/shard_map/concatenate | solution.py:376
  1.5 4.1 %collective-permute-start.2 = (bf16[128,256]{1,0:T(8,128)(2,1)S(1)}, bf16[128,256]{1,0:T(8,128)(2,1)S(1)}, u32[]{:S(2)}, u32[]{:S(2)}) collective-permute-start(bf16[128,256]{1,0:T(8,128)(2,1)S(1)} %pad_maximum_fusion.both_ref), channel_id=1, source_target_pairs={{0,8},{4,12},{8,0},{12,4},{1,9},{5,13},{9,1},{13,5},{2,10},{6,14},... | collective-permute-start | bytes 196616 | tf_op jit(solution)/shard_map/ppermute | solution.py:319
  5.6 1.6 %collective-permute-start.1 = (bf16[128,256]{1,0:T(8,128)(2,1)S(1)}, bf16[128,256]{1,0:T(8,128)(2,1)S(1)}, u32[]{:S(2)}, u32[]{:S(2)}) collective-permute-start(bf16[128,256]{1,0:T(8,128)(2,1)S(1)} %pad_maximum_fusion.both_ref), channel_id=1, source_target_pairs={{0,4},{4,0},{8,12},{12,8},{1,5},{5,1},{9,13},{13,9},{2,6},{6,2},{1... | collective-permute-start | bytes 196616 | tf_op jit(solution)/shard_map/ppermute | solution.py:319
  7.2 0.0 collective-permute-start
  7.2 0.0 copy-start.2
  7.2 0.0 copy-done
  7.2 0.6 %copy-done.2 = s32[8]{0:T(128)S(1)} copy-done((s32[8]{0:T(128)S(1)}, s32[8]{0:T(128)}, u32[]{:S(2)}) %copy-start.2) | copy-done | bytes 56
  7.8 0.0 copy-start.1
  7.8 0.9 %copy-done.1 = bf16[4,128,128]{2,1,0:T(8,128)(2,1)S(1)} copy-done((bf16[4,128,128]{2,1,0:T(8,128)(2,1)S(1)}, bf16[4,128,128]{2,1,0:T(8,128)(2,1)}, u32[]{:S(2)}) %copy-start.1) | copy-done | bytes 131096
  8.7 0.8 %shard_map.76 = (f32[128,512]{1,0:T(8,128)S(1)}, f32[128,512]{1,0:T(8,128)S(1)}, f32[8,512]{1,0:T(8,128)S(1)}, f32[8,512]{1,0:T(8,128)S(1)}) custom-call(s32[8]{0:T(128)S(1)} %copy-done.2, s32[4]{0:T(128)S(1)} %iota_xor_fusion.owner_ref, bf16[512,128]{1,0:T(8,128)(2,1)S(1)} %bitcast.7, bf16[512,128]{1,0:T(8,128)(2,1)S(1)} %bitcast.11, ...), custom_call_target="tpu_custom_call" | custom-call | flops 33554432 | bytes 524288 | tf_op jit(solution)/shard_map/pallas_call | solution.py:280
  9.6 0.0 collective-permute-done.2.both_ref.rest_2_
  9.6 0.3 %shard_map.77 = (f32[128,512]{1,0:T(8,128)S(1)}, f32[128,512]{1,0:T(8,128)S(1)}, f32[8,512]{1,0:T(8,128)S(1)}) custom-call(f32[8,512]{1,0:T(8,128)S(1)} %get-tuple-element.21.hide_ref, bf16[512,128]{1,0:T(8,128)(2,1)S(1)} %bitcast.8, bf16[512,128]{1,0:T(8,128)(2,1)S(1)} %bitcast.12, bf16[128,256]{1,0:T(8,128)(2,1)S(1)} %collective-permute-done.2.both_ref.rest_2_), custom_call_target="tpu_custom_call" | custom-call | flops 33554432 | bytes 524288 | tf_op jit(solution)/shard_map/pallas_call | solution.py:280
  9.9 0.0 collective-permute-done.1.rest_1_
  9.9 3.4 %collective-permute-done.rest_0_ = bf16[128,256]{1,0:T(8,128)(2,1)S(1)} collective-permute-done((bf16[128,256]{1,0:T(8,128)(2,1)S(1)}, bf16[128,256]{1,0:T(8,128)(2,1)S(1)}, u32[]{:S(2)}, u32[]{:S(2)}) %collective-permute-start) | collective-permute-done | bytes 65568 | tf_op jit(solution)/shard_map/ppermute | solution.py:319
  13.2 0.7 %shard_map.78 = (bf16[128,256]{1,0:T(8,128)(2,1)S(1)}, bf16[128,256]{1,0:T(8,128)(2,1)S(1)}, bf16[128,256]{1,0:T(8,128)(2,1)S(1)}, bf16[384,512]{1,0:T(8,128)(2,1)S(1)}, f32[8,512]{1,0:T(8,128)S(1)}) custom-call(f32[8,512]{1,0:T(8,128)S(1)} %get-tuple-element.21.hide_ref, bf16[512,128]{1,0:T(8,128)(2,1)S(1)} %bitcast.9, bf16[512,128]{1,0:T(8,128)(2,1)S(1)} %bitcast.13, ...), custom_call_target="tpu_custom_call" | custom-call | flops 201326592 | bytes 3145728 | tf_op jit(solution)/shard_map/pallas_call | solution.py:280
  14.0 1.3 %collective-permute-start.3 = (bf16[128,256]{1,0:T(8,128)(2,1)S(1)}, bf16[128,256]{1,0:T(8,128)(2,1)S(1)}, u32[]{:S(2)}, u32[]{:S(2)}) collective-permute-start(bf16[128,256]{1,0:T(8,128)(2,1)S(1)} %get-tuple-element.30), channel_id=1, source_target_pairs={{0,12},{4,8},{8,4},{12,0},{1,13},{5,9},{9,5},{13,1},{2,14},{6,10},... | collective-permute-start | bytes 196616 | tf_op jit(solution)/shard_map/ppermute | solution.py:360
  15.3 0.6 %collective-permute-start.4 = (bf16[128,256]{1,0:T(8,128)(2,1)S(1)}, bf16[128,256]{1,0:T(8,128)(2,1)S(1)}, u32[]{:S(2)}, u32[]{:S(2)}) collective-permute-start(bf16[128,256]{1,0:T(8,128)(2,1)S(1)} %get-tuple-element.31), channel_id=1, source_target_pairs={{0,4},{4,0},{8,12},{12,8},{1,5},{5,1},{9,13},{13,9},{2,6},{6,2},{1... | collective-permute-start | bytes 196616 | tf_op jit(solution)/shard_map/ppermute | solution.py:360
  15.9 2.5 %collective-permute-start.5 = (bf16[128,256]{1,0:T(8,128)(2,1)S(1)}, bf16[128,256]{1,0:T(8,128)(2,1)S(1)}, u32[]{:S(2)}, u32[]{:S(2)}) collective-permute-start(bf16[128,256]{1,0:T(8,128)(2,1)S(1)} %get-tuple-element.32), channel_id=1, source_target_pairs={{0,8},{4,12},{8,0},{12,4},{1,9},{5,13},{9,1},{13,5},{2,10},{6,14},... | collective-permute-start | bytes 196616 | tf_op jit(solution)/shard_map/ppermute | solution.py:360
  18.4 1.1 %shard_map.79 = (f32[128,256]{1,0:T(8,128)S(1)}, f32[512,128]{1,0:T(8,128)}) custom-call(bf16[512,128]{1,0:T(8,128)(2,1)S(1)} %bitcast.10, bf16[512,128]{1,0:T(8,128)(2,1)S(1)} %bitcast.14, f32[128,512]{1,0:T(8,128)S(1)} %get-tuple-element.19.power_ref, f32[128,512]{1,0:T(8,128)S(1)} %get-tuple-element.20.grad_ref, f32[8,512]{1,0:T(8,128)S(1)} %get-tuple-element.26.norm_ref, ...), custom_call_target="tpu_custom_call" | custom-call | flops 100663296 | bytes 1572864 | tf_op jit(solution)/shard_map/pallas_call | solution.py:280
  19.5 0.7 %collective-permute-done.3.rest_0_ = bf16[128,256]{1,0:T(8,128)(2,1)S(1)} collective-permute-done((bf16[128,256]{1,0:T(8,128)(2,1)S(1)}, bf16[128,256]{1,0:T(8,128)(2,1)S(1)}, u32[]{:S(2)}, u32[]{:S(2)}) %collective-permute-start.3) | collective-permute-done | bytes 65568 | tf_op jit(solution)/shard_map/ppermute | solution.py:360
  20.2 1.2 %collective-permute-done.4.rest_1_ = bf16[128,256]{1,0:T(8,128)(2,1)S(1)} collective-permute-done((bf16[128,256]{1,0:T(8,128)(2,1)S(1)}, bf16[128,256]{1,0:T(8,128)(2,1)S(1)}, u32[]{:S(2)}, u32[]{:S(2)}) %collective-permute-start.4) | collective-permute-done | bytes 65568 | tf_op jit(solution)/shard_map/ppermute | solution.py:360
  21.4 0.7 %collective-permute-done.5.rest_0_ = bf16[128,256]{1,0:T(8,128)(2,1)S(1)} collective-permute-done((bf16[128,256]{1,0:T(8,128)(2,1)S(1)}, bf16[128,256]{1,0:T(8,128)(2,1)S(1)}, u32[]{:S(2)}, u32[]{:S(2)}) %collective-permute-start.5) | collective-permute-done | bytes 65568 | tf_op jit(solution)/shard_map/ppermute | solution.py:360
  22.1 0.7 %shard_map.81 = (f32[128,128]{1,0:T(8,128)}, f32[128,128]{1,0:T(8,128)}) custom-call(bf16[128,256]{1,0:T(8,128)(2,1)S(1)} %pad_maximum_fusion.both_ref, f32[128,256]{1,0:T(8,128)S(1)} %shard_map.80.own_ref, bf16[128,256]{1,0:T(8,128)(2,1)S(1)} %collective-permute-done.5.rest_0_), custom_call_target="tpu_custom_call" | custom-call | tf_op jit(solution)/shard_map/pallas_call | solution.py:280
  (2 shorter events, 0.0 us)
Async XLA Ops:
  0.6 6.5 %copy-start = (bf16[4,128,128]{2,1,0:T(8,128)(2,1)S(1)}, bf16[4,128,128]{2,1,0:T(8,128)(2,1)}, u32[]{:S(2)}) copy-start(bf16[4,128,128]{2,1,0:T(8,128)(2,1)} %param.5) | copy-start | bytes 393220
  1.5 8.1 %collective-permute-start.2 = (bf16[128,256]{1,0:T(8,128)(2,1)S(1)}, bf16[128,256]{1,0:T(8,128)(2,1)S(1)}, u32[]{:S(2)}, u32[]{:S(2)}) collective-permute-start(bf16[128,256]{1,0:T(8,128)(2,1)S(1)} %pad_maximum_fusion.both_ref), channel_id=1, source_target_pairs={{0,8},{4,12},{8,0},{12,4},{1,9},{5,13},{9,1},{13,5},{2,10},{6,14},... | collective-permute-start | bytes 196616 | tf_op jit(solution)/shard_map/ppermute | solution.py:319
  5.6 4.3 %collective-permute-start.1 = (bf16[128,256]{1,0:T(8,128)(2,1)S(1)}, bf16[128,256]{1,0:T(8,128)(2,1)S(1)}, u32[]{:S(2)}, u32[]{:S(2)}) collective-permute-start(bf16[128,256]{1,0:T(8,128)(2,1)S(1)} %pad_maximum_fusion.both_ref), channel_id=1, source_target_pairs={{0,4},{4,0},{8,12},{12,8},{1,5},{5,1},{9,13},{13,9},{2,6},{6,2},{1... | collective-permute-start | bytes 196616 | tf_op jit(solution)/shard_map/ppermute | solution.py:319
  7.2 6.1 %collective-permute-start = (bf16[128,256]{1,0:T(8,128)(2,1)S(1)}, bf16[128,256]{1,0:T(8,128)(2,1)S(1)}, u32[]{:S(2)}, u32[]{:S(2)}) collective-permute-start(bf16[128,256]{1,0:T(8,128)(2,1)S(1)} %pad_maximum_fusion.both_ref), channel_id=1, source_target_pairs={{0,12},{4,8},{8,4},{12,0},{1,13},{5,9},{9,5},{13,1},{2,14},{6,10},... | collective-permute-start | bytes 196616 | tf_op jit(solution)/shard_map/ppermute | solution.py:319
  7.2 0.7 %copy-start.2 = (s32[8]{0:T(128)S(1)}, s32[8]{0:T(128)}, u32[]{:S(2)}) copy-start(s32[8]{0:T(128)} %order_ref.1) | copy-start | bytes 100
  7.8 0.9 %copy-start.1 = (bf16[4,128,128]{2,1,0:T(8,128)(2,1)S(1)}, bf16[4,128,128]{2,1,0:T(8,128)(2,1)}, u32[]{:S(2)}) copy-start(bf16[4,128,128]{2,1,0:T(8,128)(2,1)} %param.8) | copy-start | bytes 393220
  14.0 6.2 %collective-permute-start.3 = (bf16[128,256]{1,0:T(8,128)(2,1)S(1)}, bf16[128,256]{1,0:T(8,128)(2,1)S(1)}, u32[]{:S(2)}, u32[]{:S(2)}) collective-permute-start(bf16[128,256]{1,0:T(8,128)(2,1)S(1)} %get-tuple-element.30), channel_id=1, source_target_pairs={{0,12},{4,8},{8,4},{12,0},{1,13},{5,9},{9,5},{13,1},{2,14},{6,10},... | collective-permute-start | bytes 196616 | tf_op jit(solution)/shard_map/ppermute | solution.py:360
  15.3 6.1 %collective-permute-start.4 = (bf16[128,256]{1,0:T(8,128)(2,1)S(1)}, bf16[128,256]{1,0:T(8,128)(2,1)S(1)}, u32[]{:S(2)}, u32[]{:S(2)}) collective-permute-start(bf16[128,256]{1,0:T(8,128)(2,1)S(1)} %get-tuple-element.31), channel_id=1, source_target_pairs={{0,4},{4,0},{8,12},{12,8},{1,5},{5,1},{9,13},{13,9},{2,6},{6,2},{1... | collective-permute-start | bytes 196616 | tf_op jit(solution)/shard_map/ppermute | solution.py:360
  15.9 6.2 %collective-permute-start.5 = (bf16[128,256]{1,0:T(8,128)(2,1)S(1)}, bf16[128,256]{1,0:T(8,128)(2,1)S(1)}, u32[]{:S(2)}, u32[]{:S(2)}) collective-permute-start(bf16[128,256]{1,0:T(8,128)(2,1)S(1)} %get-tuple-element.32), channel_id=1, source_target_pairs={{0,8},{4,12},{8,0},{12,4},{1,9},{5,13},{9,1},{13,5},{2,10},{6,14},... | collective-permute-start | bytes 196616 | tf_op jit(solution)/shard_map/ppermute | solution.py:360

commit v2 on v0

--- a/solution.py
+++ b/solution.py
@@ -14,8 +14,8 @@
 HIDDEN = -1e30
 FEW = 8
 LOG2E = math.log2(math.e)
-KEYS_FIRST = (2, 3, 1)
-TERMS_FIRST = (3, 1, 2)
+KEYS_FIRST = (1, 2, 3)
+TERMS_FIRST = (3, 2, 1)
 
 
 def dot(a, b, dims):
@@ -117,7 +117,7 @@
     seen_refs, rest = rest[: len(late)], rest[len(late) :]
     stat_refs, rest = rest[: len(early) + 1], rest[len(early) + 1 :]
     tile_refs, rest = rest[: 2 * len(early)], rest[2 * len(early) :]
-    term_ref, soft_ref, norm_ref, low_ref = rest
+    *term_refs, soft_ref, norm_ref, low_ref = rest
     rows = seen_refs[0].shape[0]
     queries, head = query_ref.shape
     keys = jnp.concatenate([ref[:, :head] for ref in seen_refs], axis=0)
@@ -154,22 +154,11 @@
             lines = slice(place * rows, (place + 1) * rows)
             soft_ref[lines, span] = (weights * (slopes - expect)).astype(BF16)
             low_ref[lines, span] = weights.astype(BF16)
-    store_terms(soft_ref[:rows], low_ref[:rows], query_ref, ratio_ref, [term_ref])
-
-
-def store_terms(soft, low, query_ref, ratio_ref, term_refs):
-    head = query_ref.shape[1]
-    key_part = dot(soft, query_ref[...], ((1,), (0,))).astype(BF16)
-    value_part = dot(low, ratio_ref[...], ((1,), (0,))).astype(BF16)
+    key_part = dot(soft_ref[...], query_ref[...], ((1,), (0,))).astype(BF16)
+    value_part = dot(low_ref[...], ratio_ref[...], ((1,), (0,))).astype(BF16)
     for place, term_ref in enumerate(term_refs):
-        rows = term_ref.shape[0]
         term_ref[:, :head] = key_part[place * rows : (place + 1) * rows]
         term_ref[:, head:] = value_part[place * rows : (place + 1) * rows]
-
-
-def rest_kernel(query_ref, ratio_ref, soft_ref, low_ref, *term_refs):
-    rows = term_refs[0].shape[0]
-    store_terms(soft_ref[rows:], low_ref[rows:], query_ref, ratio_ref, term_refs)
 
 
 def own_kernel(factor, query_ref, ratio_ref, power_ref, grad_ref, norm_ref, both_ref, soft_ref, *rest):
@@ -254,7 +243,6 @@
     blocks = block_order.shape[0] // slots
     block_rows = rows // blocks
     shape = (blocks, block_rows)
-    swap = slots & (slots - 1) == 0
     limit = min(60 << 20, (8 << 20) + 16 * slots * rows * queries)
     params = pltpu.CompilerParams(vmem_limit_bytes=limit)
     smem = pl.BlockSpec(memory_space=pltpu.SMEM)
@@ -283,8 +271,6 @@
         )(*scalars, *arrays)
 
     def pairs(step, back):
-        if swap:
-            return [(device, device ^ step) for device in range(slots)]
         step = -step if back else step
         return [(device, (device + step) % slots) for device in range(slots)]
 
@@ -309,7 +295,7 @@
         for step in first:
             seen[step] = lax.ppermute(both, "seq", pairs(step, False))
         device = jnp.arange(slots, dtype=jnp.int32)
-        owners = mine ^ device if swap else lax.rem(mine - device + slots, slots)
+        owners = lax.rem(mine - device + slots, slots)
         power, grad, stats = {}, {}, {}
         power[0], grad[0], stats[0], hides = run(
             functools.partial(own_block_kernel, shape, scale),
@@ -330,10 +316,13 @@
                 (hides, query_rows, ratio_rows, seen[slot]),
                 2,
             )
-        low_tiles = jax.ShapeDtypeStruct((len(then) * rows, queries), BF16)
-        term_first, soft, norm, low = run(
+        *terms, soft, norm = run(
             functools.partial(late_kernel, blocks, scale, then, late, width),
-            (low_term, low_tiles, stat, low_tiles),
+            (
+                *[low_term] * len(then),
+                jax.ShapeDtypeStruct((len(then) * rows, queries), BF16),
+                stat,
+            ),
             (),
             (
                 *(hides, query_rows, ratio_rows),
@@ -342,16 +331,8 @@
                 *(one for slot in early for one in (power[slot], grad[slot])),
             ),
             4 * len(then),
-        )
-        terms = [term_first]
-        if then[1:]:
-            terms += run(
-                rest_kernel,
-                (low_term,) * len(then[1:]),
-                (),
-                (query_rows, ratio_rows, soft, low),
-                2 * len(then[1:]),
-            )
+            [pltpu.VMEM((len(then) * rows, queries), BF16)],
+        )
         for slot, one in zip(then, terms):
             got.append(lax.ppermute(one, "seq", pairs(slot, True)))
         own, query_out = run(

time: 23.2 us -> 22.2 us (0.957)
  waiting for transfers between devices: 5.92 us -> 4.23 us
  starting transfers between devices: 10.1 us -> 11.1 us
  Pallas kernels: 3.85 us -> 3.61 us
    ppermute x3, waiting for transfers between devices: 3.37 us -> 0.68 us  [few(): seen[step] = lax.ppermute(both, 'seq', pairs(step, False))]
    ppermute x3, starting transfers between devices: 5.7 us -> 7.04 us  [few(): seen[step] = lax.ppermute(both, 'seq', pairs(step, False))]
    ppermute x3, waiting for transfers between devices: 2.55 us -> 3.54 us  [few(): got.append(lax.ppermute(one, 'seq', pairs(slot, True)))]
    ppermute x3, starting transfers between devices: 4.44 us -> 4.09 us  [few(): got.append(lax.ppermute(one, 'seq', pairs(slot, True)))]
    pallas_call x6 -> x5, Pallas kernels: 3.85 us -> 3.61 us  [run(): pl.pallas_call(kernel, out_shape=outs, in_specs=[smem] * len(scalars) + [...]
  transfers between devices with their start and end apart: 6 -> 6, of which waited for: 2 -> 5; matrix products, arithmetic and copies ran while one was open for 0% -> 0% of each run, Pallas kernels for 9% -> 10%
where the time goes in v2:
time: 22.2 us; the launch traced here: 22 us
  starting transfers between devices  11.1 us (50%)
  waiting for transfers between devices  4.23 us (19%)
  Pallas kernels  3.61 us (16%)
  local copies, waits for them, and re-layouts  1.55 us (7%)
  other arithmetic  0.83 us (4%)
  between operations  0.68 us (3%)
    ppermute x3, starting transfers between devices, few(): seen[step] = lax.ppermute(both, 'seq', pairs(step, False))  7.04 us
    ppermute x3, starting transfers between devices, few(): got.append(lax.ppermute(one, 'seq', pairs(slot, True)))  4.09 us
    pallas_call x5, Pallas kernels, run(): pl.pallas_call(kernel, out_shape=outs, in_specs=[smem] * len(scalars) + [...  3.61 us
    ppermute x3, waiting for transfers between devices, few(): got.append(lax.ppermute(one, 'seq', pairs(slot, True)))  3.54 us
    unnamed x6, local copies, waits for them, and re-layouts  1.55 us
    concatenate x1, other arithmetic, one_head(): both = jnp.concatenate((key_rows, value_rows), axis=1)  0.82 us
    ppermute x3, waiting for transfers between devices, few(): seen[step] = lax.ppermute(both, 'seq', pairs(step, False))  0.68 us
  transfers between devices with their start and end apart: 6, of which 5 were waited for; matrix products, arithmetic and copies ran while one was open for 0% of the time, Pallas kernels for 10%

profile of v2, /device:TPU:0, one launch (start us, length us, event | category | flops | bytes accessed | tf_op | source)
XLA Modules:
  0.0 22.0 jit_solution(1767516035051073188)
XLA Ops:
  0.6 0.0 copy-start
  0.6 0.8 %pad_maximum_fusion.both_ref = bf16[128,256]{1,0:T(8,128)(2,1)S(1)} fusion(bf16[128,128]{1,0:T(8,128)(2,1)} %bitcast.15, bf16[128,128]{1,0:T(8,128)(2,1)} %bitcast.16), kind=kLoop, calls=%fused_computation | loop fusion | flops 131072 | bytes 131072 | tf_op jit(solution)/shard_map/concatenate | solution.py:351
  1.5 3.1 %collective-permute-start.2 = (bf16[128,256]{1,0:T(8,128)(2,1)S(1)}, bf16[128,256]{1,0:T(8,128)(2,1)S(1)}, u32[]{:S(2)}, u32[]{:S(2)}) collective-permute-start(bf16[128,256]{1,0:T(8,128)(2,1)S(1)} %pad_maximum_fusion.both_ref), channel_id=1, source_target_pairs={{0,4},{4,8},{8,12},{12,0},{1,5},{5,9},{9,13},{13,1},{2,6},{6,10},{... | collective-permute-start | bytes 196616 | tf_op jit(solution)/shard_map/ppermute | solution.py:296
  4.6 2.6 %collective-permute-start.1 = (bf16[128,256]{1,0:T(8,128)(2,1)S(1)}, bf16[128,256]{1,0:T(8,128)(2,1)S(1)}, u32[]{:S(2)}, u32[]{:S(2)}) collective-permute-start(bf16[128,256]{1,0:T(8,128)(2,1)S(1)} %pad_maximum_fusion.both_ref), channel_id=1, source_target_pairs={{0,8},{4,12},{8,0},{12,4},{1,9},{5,13},{9,1},{13,5},{2,10},{6,14},... | collective-permute-start | bytes 196616 | tf_op jit(solution)/shard_map/ppermute | solution.py:296
  7.1 1.3 %collective-permute-start = (bf16[128,256]{1,0:T(8,128)(2,1)S(1)}, bf16[128,256]{1,0:T(8,128)(2,1)S(1)}, u32[]{:S(2)}, u32[]{:S(2)}) collective-permute-start(bf16[128,256]{1,0:T(8,128)(2,1)S(1)} %pad_maximum_fusion.both_ref), channel_id=1, source_target_pairs={{0,12},{4,0},{8,4},{12,8},{1,13},{5,1},{9,5},{13,9},{2,14},{6,2},{... | collective-permute-start | bytes 196616 | tf_op jit(solution)/shard_map/ppermute | solution.py:296
  8.5 0.0 copy-start.2
  8.5 0.0 copy-done
  8.5 0.6 %copy-done.2 = s32[8]{0:T(128)S(1)} copy-done((s32[8]{0:T(128)S(1)}, s32[8]{0:T(128)}, u32[]{:S(2)}) %copy-start.2) | copy-done | bytes 56
  9.2 0.0 copy-start.1
  9.2 0.9 %copy-done.1 = bf16[4,128,128]{2,1,0:T(8,128)(2,1)S(1)} copy-done((bf16[4,128,128]{2,1,0:T(8,128)(2,1)S(1)}, bf16[4,128,128]{2,1,0:T(8,128)(2,1)}, u32[]{:S(2)}) %copy-start.1) | copy-done | bytes 131096
  10.1 0.8 %shard_map.76 = (f32[128,512]{1,0:T(8,128)S(1)}, f32[128,512]{1,0:T(8,128)S(1)}, f32[8,512]{1,0:T(8,128)S(1)}, f32[8,512]{1,0:T(8,128)S(1)}) custom-call(s32[8]{0:T(128)S(1)} %copy-done.2, s32[4]{0:T(128)S(1)} %compare_select_fusion.owner_ref, bf16[512,128]{1,0:T(8,128)(2,1)S(1)} %bitcast.7, bf16[512,128]{1,0:T(8,128)(2,1)S(1)} %bitcast.11, ...), custom_call_target="tpu_custom_call" | custom-call | flops 33554432 | bytes 524288 | tf_op jit(solution)/shard_map/pallas_call | solution.py:259
  10.9 0.0 collective-permute-done.2.both_ref.rest_2_
  10.9 0.3 %shard_map.77 = (f32[128,512]{1,0:T(8,128)S(1)}, f32[128,512]{1,0:T(8,128)S(1)}, f32[8,512]{1,0:T(8,128)S(1)}) custom-call(f32[8,512]{1,0:T(8,128)S(1)} %get-tuple-element.21.hide_ref, bf16[512,128]{1,0:T(8,128)(2,1)S(1)} %bitcast.8, bf16[512,128]{1,0:T(8,128)(2,1)S(1)} %bitcast.12, bf16[128,256]{1,0:T(8,128)(2,1)S(1)} %collective-permute-done.2.both_ref.rest_2_), custom_call_target="tpu_custom_call" | custom-call | flops 33554432 | bytes 524288 | tf_op jit(solution)/shard_map/pallas_call | solution.py:259
  11.2 0.5 %collective-permute-done.1.rest_1_ = bf16[128,256]{1,0:T(8,128)(2,1)S(1)} collective-permute-done((bf16[128,256]{1,0:T(8,128)(2,1)S(1)}, bf16[128,256]{1,0:T(8,128)(2,1)S(1)}, u32[]{:S(2)}, u32[]{:S(2)}) %collective-permute-start.1) | collective-permute-done | bytes 65568 | tf_op jit(solution)/shard_map/ppermute | solution.py:296
  11.6 0.2 %collective-permute-done.rest_0_ = bf16[128,256]{1,0:T(8,128)(2,1)S(1)} collective-permute-done((bf16[128,256]{1,0:T(8,128)(2,1)S(1)}, bf16[128,256]{1,0:T(8,128)(2,1)S(1)}, u32[]{:S(2)}, u32[]{:S(2)}) %collective-permute-start) | collective-permute-done | bytes 65568 | tf_op jit(solution)/shard_map/ppermute | solution.py:296
  11.9 0.7 %shard_map.78 = (bf16[128,256]{1,0:T(8,128)(2,1)S(1)}, bf16[128,256]{1,0:T(8,128)(2,1)S(1)}, bf16[128,256]{1,0:T(8,128)(2,1)S(1)}, bf16[384,512]{1,0:T(8,128)(2,1)S(1)}, f32[8,512]{1,0:T(8,128)S(1)}) custom-call(f32[8,512]{1,0:T(8,128)S(1)} %get-tuple-element.21.hide_ref, bf16[512,128]{1,0:T(8,128)(2,1)S(1)} %bitcast.9, bf16[512,128]{1,0:T(8,128)(2,1)S(1)} %bitcast.13, ...), custom_call_target="tpu_custom_call" | custom-call | flops 201326592 | bytes 3145728 | tf_op jit(solution)/shard_map/pallas_call | solution.py:259
  12.6 1.6 %collective-permute-start.3 = (bf16[128,256]{1,0:T(8,128)(2,1)S(1)}, bf16[128,256]{1,0:T(8,128)(2,1)S(1)}, u32[]{:S(2)}, u32[]{:S(2)}) collective-permute-start(bf16[128,256]{1,0:T(8,128)(2,1)S(1)} %get-tuple-element.30), channel_id=1, source_target_pairs={{0,4},{4,8},{8,12},{12,0},{1,5},{5,9},{9,13},{13,1},{2,6},{6,10},{... | collective-permute-start | bytes 196616 | tf_op jit(solution)/shard_map/ppermute | solution.py:337
  14.3 2.0 %collective-permute-start.4 = (bf16[128,256]{1,0:T(8,128)(2,1)S(1)}, bf16[128,256]{1,0:T(8,128)(2,1)S(1)}, u32[]{:S(2)}, u32[]{:S(2)}) collective-permute-start(bf16[128,256]{1,0:T(8,128)(2,1)S(1)} %get-tuple-element.31), channel_id=1, source_target_pairs={{0,8},{4,12},{8,0},{12,4},{1,9},{5,13},{9,1},{13,5},{2,10},{6,14},... | collective-permute-start | bytes 196616 | tf_op jit(solution)/shard_map/ppermute | solution.py:337
  16.3 0.4 %collective-permute-start.5 = (bf16[128,256]{1,0:T(8,128)(2,1)S(1)}, bf16[128,256]{1,0:T(8,128)(2,1)S(1)}, u32[]{:S(2)}, u32[]{:S(2)}) collective-permute-start(bf16[128,256]{1,0:T(8,128)(2,1)S(1)} %get-tuple-element.32), channel_id=1, source_target_pairs={{0,12},{4,0},{8,4},{12,8},{1,13},{5,1},{9,5},{13,9},{2,14},{6,2},{... | collective-permute-start | bytes 196616 | tf_op jit(solution)/shard_map/ppermute | solution.py:337
  16.7 1.1 %shard_map.79 = (f32[128,256]{1,0:T(8,128)S(1)}, f32[512,128]{1,0:T(8,128)}) custom-call(bf16[512,128]{1,0:T(8,128)(2,1)S(1)} %bitcast.10, bf16[512,128]{1,0:T(8,128)(2,1)S(1)} %bitcast.14, f32[128,512]{1,0:T(8,128)S(1)} %get-tuple-element.19.power_ref, f32[128,512]{1,0:T(8,128)S(1)} %get-tuple-element.20.grad_ref, f32[8,512]{1,0:T(8,128)S(1)} %get-tuple-element.26.norm_ref, ...), custom_call_target="tpu_custom_call" | custom-call | flops 100663296 | bytes 1572864 | tf_op jit(solution)/shard_map/pallas_call | solution.py:259
  17.8 1.1 %collective-permute-done.3.rest_0_ = bf16[128,256]{1,0:T(8,128)(2,1)S(1)} collective-permute-done((bf16[128,256]{1,0:T(8,128)(2,1)S(1)}, bf16[128,256]{1,0:T(8,128)(2,1)S(1)}, u32[]{:S(2)}, u32[]{:S(2)}) %collective-permute-start.3) | collective-permute-done | bytes 65568 | tf_op jit(solution)/shard_map/ppermute | solution.py:337
  18.9 2.1 %collective-permute-done.4.rest_1_ = bf16[128,256]{1,0:T(8,128)(2,1)S(1)} collective-permute-done((bf16[128,256]{1,0:T(8,128)(2,1)S(1)}, bf16[128,256]{1,0:T(8,128)(2,1)S(1)}, u32[]{:S(2)}, u32[]{:S(2)}) %collective-permute-start.4) | collective-permute-done | bytes 65568 | tf_op jit(solution)/shard_map/ppermute | solution.py:337
  21.0 0.4 %collective-permute-done.5.rest_2_ = bf16[128,256]{1,0:T(8,128)(2,1)S(1)} collective-permute-done((bf16[128,256]{1,0:T(8,128)(2,1)S(1)}, bf16[128,256]{1,0:T(8,128)(2,1)S(1)}, u32[]{:S(2)}, u32[]{:S(2)}) %collective-permute-start.5) | collective-permute-done | bytes 65568 | tf_op jit(solution)/shard_map/ppermute | solution.py:337
  21.3 0.7 %shard_map.80 = (f32[128,128]{1,0:T(8,128)}, f32[128,128]{1,0:T(8,128)}) custom-call(bf16[128,256]{1,0:T(8,128)(2,1)S(1)} %pad_maximum_fusion.both_ref, f32[128,256]{1,0:T(8,128)S(1)} %get-tuple-element.29.own_ref, bf16[128,256]{1,0:T(8,128)(2,1)S(1)} %collective-permute-done.3.rest_0_, bf16[128,256]{1,0:T(8,128)(2,1)S(1)} %collective-permute-done.4.rest_1_, ...), custom_call_target="tpu_custom_call" | custom-call | tf_op jit(solution)/shard_map/pallas_call | solution.py:259
  (1 shorter events, 0.0 us)
Async XLA Ops:
  0.6 7.9 %copy-start = (bf16[4,128,128]{2,1,0:T(8,128)(2,1)S(1)}, bf16[4,128,128]{2,1,0:T(8,128)(2,1)}, u32[]{:S(2)}) copy-start(bf16[4,128,128]{2,1,0:T(8,128)(2,1)} %param.5) | copy-start | bytes 393220
  1.5 9.4 %collective-permute-start.2 = (bf16[128,256]{1,0:T(8,128)(2,1)S(1)}, bf16[128,256]{1,0:T(8,128)(2,1)S(1)}, u32[]{:S(2)}, u32[]{:S(2)}) collective-permute-start(bf16[128,256]{1,0:T(8,128)(2,1)S(1)} %pad_maximum_fusion.both_ref), channel_id=1, source_target_pairs={{0,4},{4,8},{8,12},{12,0},{1,5},{5,9},{9,13},{13,1},{2,6},{6,10},{... | collective-permute-start | bytes 196616 | tf_op jit(solution)/shard_map/ppermute | solution.py:296
  4.6 7.1 %collective-permute-start.1 = (bf16[128,256]{1,0:T(8,128)(2,1)S(1)}, bf16[128,256]{1,0:T(8,128)(2,1)S(1)}, u32[]{:S(2)}, u32[]{:S(2)}) collective-permute-start(bf16[128,256]{1,0:T(8,128)(2,1)S(1)} %pad_maximum_fusion.both_ref), channel_id=1, source_target_pairs={{0,8},{4,12},{8,0},{12,4},{1,9},{5,13},{9,1},{13,5},{2,10},{6,14},... | collective-permute-start | bytes 196616 | tf_op jit(solution)/shard_map/ppermute | solution.py:296
  7.1 4.7 %collective-permute-start = (bf16[128,256]{1,0:T(8,128)(2,1)S(1)}, bf16[128,256]{1,0:T(8,128)(2,1)S(1)}, u32[]{:S(2)}, u32[]{:S(2)}) collective-permute-start(bf16[128,256]{1,0:T(8,128)(2,1)S(1)} %pad_maximum_fusion.both_ref), channel_id=1, source_target_pairs={{0,12},{4,0},{8,4},{12,8},{1,13},{5,1},{9,5},{13,9},{2,14},{6,2},{... | collective-permute-start | bytes 196616 | tf_op jit(solution)/shard_map/ppermute | solution.py:296
  8.5 0.7 %copy-start.2 = (s32[8]{0:T(128)S(1)}, s32[8]{0:T(128)}, u32[]{:S(2)}) copy-start(s32[8]{0:T(128)} %order_ref.1) | copy-start | bytes 100
  9.2 0.9 %copy-start.1 = (bf16[4,128,128]{2,1,0:T(8,128)(2,1)S(1)}, bf16[4,128,128]{2,1,0:T(8,128)(2,1)}, u32[]{:S(2)}) copy-start(bf16[4,128,128]{2,1,0:T(8,128)(2,1)} %param.8) | copy-start | bytes 393220
  12.6 6.3 %collective-permute-start.3 = (bf16[128,256]{1,0:T(8,128)(2,1)S(1)}, bf16[128,256]{1,0:T(8,128)(2,1)S(1)}, u32[]{:S(2)}, u32[]{:S(2)}) collective-permute-start(bf16[128,256]{1,0:T(8,128)(2,1)S(1)} %get-tuple-element.30), channel_id=1, source_target_pairs={{0,4},{4,8},{8,12},{12,0},{1,5},{5,9},{9,13},{13,1},{2,6},{6,10},{... | collective-permute-start | bytes 196616 | tf_op jit(solution)/shard_map/ppermute | solution.py:337
  14.3 6.7 %collective-permute-start.4 = (bf16[128,256]{1,0:T(8,128)(2,1)S(1)}, bf16[128,256]{1,0:T(8,128)(2,1)S(1)}, u32[]{:S(2)}, u32[]{:S(2)}) collective-permute-start(bf16[128,256]{1,0:T(8,128)(2,1)S(1)} %get-tuple-element.31), channel_id=1, source_target_pairs={{0,8},{4,12},{8,0},{12,4},{1,9},{5,13},{9,1},{13,5},{2,10},{6,14},... | collective-permute-start | bytes 196616 | tf_op jit(solution)/shard_map/ppermute | solution.py:337
  16.3 5.1 %collective-permute-start.5 = (bf16[128,256]{1,0:T(8,128)(2,1)S(1)}, bf16[128,256]{1,0:T(8,128)(2,1)S(1)}, u32[]{:S(2)}, u32[]{:S(2)}) collective-permute-start(bf16[128,256]{1,0:T(8,128)(2,1)S(1)} %get-tuple-element.32), channel_id=1, source_target_pairs={{0,12},{4,0},{8,4},{12,8},{1,13},{5,1},{9,5},{13,9},{2,14},{6,2},{... | collective-permute-start | bytes 196616 | tf_op jit(solution)/shard_map/ppermute | solution.py:337

commit v3 on v2

--- a/solution.py
+++ b/solution.py
@@ -14,7 +14,7 @@
 HIDDEN = -1e30
 FEW = 8
 LOG2E = math.log2(math.e)
-KEYS_FIRST = (1, 2, 3)
+KEYS_FIRST = (3, 1, 2)
 TERMS_FIRST = (3, 2, 1)
 
 
@@ -243,6 +243,7 @@
     blocks = block_order.shape[0] // slots
     block_rows = rows // blocks
     shape = (blocks, block_rows)
+    swap = slots & (slots - 1) == 0
     limit = min(60 << 20, (8 << 20) + 16 * slots * rows * queries)
     params = pltpu.CompilerParams(vmem_limit_bytes=limit)
     smem = pl.BlockSpec(memory_space=pltpu.SMEM)
@@ -271,6 +272,8 @@
         )(*scalars, *arrays)
 
     def pairs(step, back):
+        if swap:
+            return [(device, device ^ step) for device in range(slots)]
         step = -step if back else step
         return [(device, (device + step) % slots) for device in range(slots)]
 
@@ -295,7 +298,7 @@
         for step in first:
             seen[step] = lax.ppermute(both, "seq", pairs(step, False))
         device = jnp.arange(slots, dtype=jnp.int32)
-        owners = lax.rem(mine - device + slots, slots)
+        owners = mine ^ device if swap else lax.rem(mine - device + slots, slots)
         power, grad, stats = {}, {}, {}
         power[0], grad[0], stats[0], hides = run(
             functools.partial(own_block_kernel, shape, scale),

time: 22.2 us -> 22.1 us (level)
  starting transfers between devices: 11.1 us -> 10.2 us
  waiting for transfers between devices: 4.23 us -> 5.02 us
    ppermute x3, waiting for transfers between devices: 0.68 us -> 2.31 us  [few(): seen[step] = lax.ppermute(both, 'seq', pairs(step, False))]
    ppermute x3, starting transfers between devices: 7.04 us -> 5.78 us  [few(): seen[step] = lax.ppermute(both, 'seq', pairs(step, False))]
    ppermute x3, waiting for transfers between devices: 3.54 us -> 2.7 us  [few(): got.append(lax.ppermute(one, 'seq', pairs(slot, True)))]
    ppermute x3, starting transfers between devices: 4.09 us -> 4.45 us  [few(): got.append(lax.ppermute(one, 'seq', pairs(slot, True)))]
  transfers between devices with their start and end apart: 6 -> 6, of which waited for: 5 -> 4; matrix products, arithmetic and copies ran while one was open for 0% -> 0% of each run, Pallas kernels for 10% -> 10%
where the time goes in v3:
time: 22.1 us; the launch traced here: 22 us
  starting transfers between devices  10.2 us (46%)
  waiting for transfers between devices  5.02 us (23%)
  Pallas kernels  3.67 us (17%)
  local copies, waits for them, and re-layouts  1.56 us (7%)
  other arithmetic  0.82 us (4%)
  between operations  0.68 us (3%)
    ppermute x3, starting transfers between devices, few(): seen[step] = lax.ppermute(both, 'seq', pairs(step, False))  5.78 us
    ppermute x3, starting transfers between devices, few(): got.append(lax.ppermute(one, 'seq', pairs(slot, True)))  4.45 us
    pallas_call x5, Pallas kernels, run(): pl.pallas_call(kernel, out_shape=outs, in_specs=[smem] * len(scalars) + [...  3.67 us
    ppermute x3, waiting for transfers between devices, few(): got.append(lax.ppermute(one, 'seq', pairs(slot, True)))  2.7 us
    ppermute x3, waiting for transfers between devices, few(): seen[step] = lax.ppermute(both, 'seq', pairs(step, False))  2.31 us
    unnamed x6, local copies, waits for them, and re-layouts  1.56 us
    concatenate x1, other arithmetic, one_head(): both = jnp.concatenate((key_rows, value_rows), axis=1)  0.82 us
  transfers between devices with their start and end apart: 6, of which 4 were waited for; matrix products, arithmetic and copies ran while one was open for 0% of the time, Pallas kernels for 10%

profile of v3, /device:TPU:0, one launch (start us, length us, event | category | flops | bytes accessed | tf_op | source)
XLA Modules:
  0.0 22.0 jit_solution(5238368775637972615)
XLA Ops:
  0.6 0.0 copy-start
  0.6 0.8 %pad_maximum_fusion.both_ref = bf16[128,256]{1,0:T(8,128)(2,1)S(1)} fusion(bf16[128,128]{1,0:T(8,128)(2,1)} %bitcast.15, bf16[128,128]{1,0:T(8,128)(2,1)} %bitcast.16), kind=kLoop, calls=%fused_computation | loop fusion | flops 131072 | bytes 131072 | tf_op jit(solution)/shard_map/concatenate | solution.py:354
  1.5 5.1 %collective-permute-start.2 = (bf16[128,256]{1,0:T(8,128)(2,1)S(1)}, bf16[128,256]{1,0:T(8,128)(2,1)S(1)}, u32[]{:S(2)}, u32[]{:S(2)}) collective-permute-start(bf16[128,256]{1,0:T(8,128)(2,1)S(1)} %pad_maximum_fusion.both_ref), channel_id=1, source_target_pairs={{0,12},{4,8},{8,4},{12,0},{1,13},{5,9},{9,5},{13,1},{2,14},{6,10},... | collective-permute-start | bytes 196616 | tf_op jit(solution)/shard_map/ppermute | solution.py:299
  6.6 0.0 collective-permute-start.1
  6.6 0.6 %collective-permute-start = (bf16[128,256]{1,0:T(8,128)(2,1)S(1)}, bf16[128,256]{1,0:T(8,128)(2,1)S(1)}, u32[]{:S(2)}, u32[]{:S(2)}) collective-permute-start(bf16[128,256]{1,0:T(8,128)(2,1)S(1)} %pad_maximum_fusion.both_ref), channel_id=1, source_target_pairs={{0,8},{4,12},{8,0},{12,4},{1,9},{5,13},{9,1},{13,5},{2,10},{6,14},... | collective-permute-start | bytes 196616 | tf_op jit(solution)/shard_map/ppermute | solution.py:299
  7.2 0.0 copy-start.2
  7.2 0.0 copy-done
  7.2 0.7 %copy-done.2 = s32[8]{0:T(128)S(1)} copy-done((s32[8]{0:T(128)S(1)}, s32[8]{0:T(128)}, u32[]{:S(2)}) %copy-start.2) | copy-done | bytes 56
  7.9 0.0 copy-start.1
  7.9 0.9 %copy-done.1 = bf16[4,128,128]{2,1,0:T(8,128)(2,1)S(1)} copy-done((bf16[4,128,128]{2,1,0:T(8,128)(2,1)S(1)}, bf16[4,128,128]{2,1,0:T(8,128)(2,1)}, u32[]{:S(2)}) %copy-start.1) | copy-done | bytes 131096
  8.8 0.8 %shard_map.76 = (f32[128,512]{1,0:T(8,128)S(1)}, f32[128,512]{1,0:T(8,128)S(1)}, f32[8,512]{1,0:T(8,128)S(1)}, f32[8,512]{1,0:T(8,128)S(1)}) custom-call(s32[8]{0:T(128)S(1)} %copy-done.2, s32[4]{0:T(128)S(1)} %iota_xor_fusion.owner_ref, bf16[512,128]{1,0:T(8,128)(2,1)S(1)} %bitcast.7, bf16[512,128]{1,0:T(8,128)(2,1)S(1)} %bitcast.11, ...), custom_call_target="tpu_custom_call" | custom-call | flops 33554432 | bytes 524288 | tf_op jit(solution)/shard_map/pallas_call | solution.py:260
  9.6 0.0 collective-permute-done.2.both_ref.rest_0_
  9.6 0.3 %shard_map.77 = (f32[128,512]{1,0:T(8,128)S(1)}, f32[128,512]{1,0:T(8,128)S(1)}, f32[8,512]{1,0:T(8,128)S(1)}) custom-call(f32[8,512]{1,0:T(8,128)S(1)} %get-tuple-element.21.hide_ref, bf16[512,128]{1,0:T(8,128)(2,1)S(1)} %bitcast.8, bf16[512,128]{1,0:T(8,128)(2,1)S(1)} %bitcast.12, bf16[128,256]{1,0:T(8,128)(2,1)S(1)} %collective-permute-done.2.both_ref.rest_0_), custom_call_target="tpu_custom_call" | custom-call | flops 33554432 | bytes 524288 | tf_op jit(solution)/shard_map/pallas_call | solution.py:260
  9.9 1.3 %collective-permute-done.1.rest_1_.rest_2_ = bf16[128,256]{1,0:T(8,128)(2,1)S(1)} collective-permute-done((bf16[128,256]{1,0:T(8,128)(2,1)S(1)}, bf16[128,256]{1,0:T(8,128)(2,1)S(1)}, u32[]{:S(2)}, u32[]{:S(2)}) %collective-permute-start.1) | collective-permute-done | bytes 65568 | tf_op jit(solution)/shard_map/ppermute | solution.py:299
  11.3 1.0 %collective-permute-done.rest_0_.rest_1_ = bf16[128,256]{1,0:T(8,128)(2,1)S(1)} collective-permute-done((bf16[128,256]{1,0:T(8,128)(2,1)S(1)}, bf16[128,256]{1,0:T(8,128)(2,1)S(1)}, u32[]{:S(2)}, u32[]{:S(2)}) %collective-permute-start) | collective-permute-done | bytes 65568 | tf_op jit(solution)/shard_map/ppermute | solution.py:299
  12.2 0.8 %shard_map.78 = (bf16[128,256]{1,0:T(8,128)(2,1)S(1)}, bf16[128,256]{1,0:T(8,128)(2,1)S(1)}, bf16[128,256]{1,0:T(8,128)(2,1)S(1)}, bf16[384,512]{1,0:T(8,128)(2,1)S(1)}, f32[8,512]{1,0:T(8,128)S(1)}) custom-call(f32[8,512]{1,0:T(8,128)S(1)} %get-tuple-element.21.hide_ref, bf16[512,128]{1,0:T(8,128)(2,1)S(1)} %bitcast.9, bf16[512,128]{1,0:T(8,128)(2,1)S(1)} %bitcast.13, ...), custom_call_target="tpu_custom_call" | custom-call | flops 201326592 | bytes 3145728 | tf_op jit(solution)/shard_map/pallas_call | solution.py:260
  13.1 2.9 %collective-permute-start.3 = (bf16[128,256]{1,0:T(8,128)(2,1)S(1)}, bf16[128,256]{1,0:T(8,128)(2,1)S(1)}, u32[]{:S(2)}, u32[]{:S(2)}) collective-permute-start(bf16[128,256]{1,0:T(8,128)(2,1)S(1)} %get-tuple-element.30), channel_id=1, source_target_pairs={{0,12},{4,8},{8,4},{12,0},{1,13},{5,9},{9,5},{13,1},{2,14},{6,10},... | collective-permute-start | bytes 196616 | tf_op jit(solution)/shard_map/ppermute | solution.py:340
  16.0 0.2 collective-permute-start.4
  16.1 1.4 %collective-permute-start.5 = (bf16[128,256]{1,0:T(8,128)(2,1)S(1)}, bf16[128,256]{1,0:T(8,128)(2,1)S(1)}, u32[]{:S(2)}, u32[]{:S(2)}) collective-permute-start(bf16[128,256]{1,0:T(8,128)(2,1)S(1)} %get-tuple-element.32), channel_id=1, source_target_pairs={{0,4},{4,0},{8,12},{12,8},{1,5},{5,1},{9,13},{13,9},{2,6},{6,2},{1... | collective-permute-start | bytes 196616 | tf_op jit(solution)/shard_map/ppermute | solution.py:340
  17.5 1.1 %shard_map.79 = (f32[128,256]{1,0:T(8,128)S(1)}, f32[512,128]{1,0:T(8,128)}) custom-call(bf16[512,128]{1,0:T(8,128)(2,1)S(1)} %bitcast.10, bf16[512,128]{1,0:T(8,128)(2,1)S(1)} %bitcast.14, f32[128,512]{1,0:T(8,128)S(1)} %get-tuple-element.19.power_ref, f32[128,512]{1,0:T(8,128)S(1)} %get-tuple-element.20.grad_ref, f32[8,512]{1,0:T(8,128)S(1)} %get-tuple-element.26.norm_ref, ...), custom_call_target="tpu_custom_call" | custom-call | flops 100663296 | bytes 1572864 | tf_op jit(solution)/shard_map/pallas_call | solution.py:260
  18.6 0.8 %collective-permute-done.3.rest_0_ = bf16[128,256]{1,0:T(8,128)(2,1)S(1)} collective-permute-done((bf16[128,256]{1,0:T(8,128)(2,1)S(1)}, bf16[128,256]{1,0:T(8,128)(2,1)S(1)}, u32[]{:S(2)}, u32[]{:S(2)}) %collective-permute-start.3) | collective-permute-done | bytes 65568 | tf_op jit(solution)/shard_map/ppermute | solution.py:340
  19.4 1.9 %collective-permute-done.4.rest_1_ = bf16[128,256]{1,0:T(8,128)(2,1)S(1)} collective-permute-done((bf16[128,256]{1,0:T(8,128)(2,1)S(1)}, bf16[128,256]{1,0:T(8,128)(2,1)S(1)}, u32[]{:S(2)}, u32[]{:S(2)}) %collective-permute-start.4) | collective-permute-done | bytes 65568 | tf_op jit(solution)/shard_map/ppermute | solution.py:340
  21.3 0.0 collective-permute-done.5.rest_2_
  21.3 0.7 %shard_map.80 = (f32[128,128]{1,0:T(8,128)}, f32[128,128]{1,0:T(8,128)}) custom-call(bf16[128,256]{1,0:T(8,128)(2,1)S(1)} %pad_maximum_fusion.both_ref, f32[128,256]{1,0:T(8,128)S(1)} %get-tuple-element.29.own_ref, bf16[128,256]{1,0:T(8,128)(2,1)S(1)} %collective-permute-done.3.rest_0_, bf16[128,256]{1,0:T(8,128)(2,1)S(1)} %collective-permute-done.4.rest_1_, ...), custom_call_target="tpu_custom_call" | custom-call | tf_op jit(solution)/shard_map/pallas_call | solution.py:260
  (1 shorter events, 0.0 us)
Async XLA Ops:
  0.6 6.6 %copy-start = (bf16[4,128,128]{2,1,0:T(8,128)(2,1)S(1)}, bf16[4,128,128]{2,1,0:T(8,128)(2,1)}, u32[]{:S(2)}) copy-start(bf16[4,128,128]{2,1,0:T(8,128)(2,1)} %param.5) | copy-start | bytes 393220
  1.5 8.2 %collective-permute-start.2 = (bf16[128,256]{1,0:T(8,128)(2,1)S(1)}, bf16[128,256]{1,0:T(8,128)(2,1)S(1)}, u32[]{:S(2)}, u32[]{:S(2)}) collective-permute-start(bf16[128,256]{1,0:T(8,128)(2,1)S(1)} %pad_maximum_fusion.both_ref), channel_id=1, source_target_pairs={{0,12},{4,8},{8,4},{12,0},{1,13},{5,9},{9,5},{13,1},{2,14},{6,10},... | collective-permute-start | bytes 196616 | tf_op jit(solution)/shard_map/ppermute | solution.py:299
  6.6 4.7 %collective-permute-start.1 = (bf16[128,256]{1,0:T(8,128)(2,1)S(1)}, bf16[128,256]{1,0:T(8,128)(2,1)S(1)}, u32[]{:S(2)}, u32[]{:S(2)}) collective-permute-start(bf16[128,256]{1,0:T(8,128)(2,1)S(1)} %pad_maximum_fusion.both_ref), channel_id=1, source_target_pairs={{0,4},{4,0},{8,12},{12,8},{1,5},{5,1},{9,13},{13,9},{2,6},{6,2},{1... | collective-permute-start | bytes 196616 | tf_op jit(solution)/shard_map/ppermute | solution.py:299
  6.6 5.6 %collective-permute-start = (bf16[128,256]{1,0:T(8,128)(2,1)S(1)}, bf16[128,256]{1,0:T(8,128)(2,1)S(1)}, u32[]{:S(2)}, u32[]{:S(2)}) collective-permute-start(bf16[128,256]{1,0:T(8,128)(2,1)S(1)} %pad_maximum_fusion.both_ref), channel_id=1, source_target_pairs={{0,8},{4,12},{8,0},{12,4},{1,9},{5,13},{9,1},{13,5},{2,10},{6,14},... | collective-permute-start | bytes 196616 | tf_op jit(solution)/shard_map/ppermute | solution.py:299
  7.2 0.7 %copy-start.2 = (s32[8]{0:T(128)S(1)}, s32[8]{0:T(128)}, u32[]{:S(2)}) copy-start(s32[8]{0:T(128)} %order_ref.1) | copy-start | bytes 100
  7.9 0.9 %copy-start.1 = (bf16[4,128,128]{2,1,0:T(8,128)(2,1)S(1)}, bf16[4,128,128]{2,1,0:T(8,128)(2,1)}, u32[]{:S(2)}) copy-start(bf16[4,128,128]{2,1,0:T(8,128)(2,1)} %param.8) | copy-start | bytes 393220
  13.1 6.4 %collective-permute-start.3 = (bf16[128,256]{1,0:T(8,128)(2,1)S(1)}, bf16[128,256]{1,0:T(8,128)(2,1)S(1)}, u32[]{:S(2)}, u32[]{:S(2)}) collective-permute-start(bf16[128,256]{1,0:T(8,128)(2,1)S(1)} %get-tuple-element.30), channel_id=1, source_target_pairs={{0,12},{4,8},{8,4},{12,0},{1,13},{5,9},{9,5},{13,1},{2,14},{6,10},... | collective-permute-start | bytes 196616 | tf_op jit(solution)/shard_map/ppermute | solution.py:340
  16.0 5.3 %collective-permute-start.4 = (bf16[128,256]{1,0:T(8,128)(2,1)S(1)}, bf16[128,256]{1,0:T(8,128)(2,1)S(1)}, u32[]{:S(2)}, u32[]{:S(2)}) collective-permute-start(bf16[128,256]{1,0:T(8,128)(2,1)S(1)} %get-tuple-element.31), channel_id=1, source_target_pairs={{0,8},{4,12},{8,0},{12,4},{1,9},{5,13},{9,1},{13,5},{2,10},{6,14},... | collective-permute-start | bytes 196616 | tf_op jit(solution)/shard_map/ppermute | solution.py:340
  16.1 5.2 %collective-permute-start.5 = (bf16[128,256]{1,0:T(8,128)(2,1)S(1)}, bf16[128,256]{1,0:T(8,128)(2,1)S(1)}, u32[]{:S(2)}, u32[]{:S(2)}) collective-permute-start(bf16[128,256]{1,0:T(8,128)(2,1)S(1)} %get-tuple-element.32), channel_id=1, source_target_pairs={{0,4},{4,0},{8,12},{12,8},{1,5},{5,1},{9,13},{13,9},{2,6},{6,2},{1... | collective-permute-start | bytes 196616 | tf_op jit(solution)/shard_map/ppermute | solution.py:340
